TPU v7x, 128 devices: a whole 4x4x4 slice. The times are simulated.
128 devices in a mesh: ctx: 32 (over y, z_hi, x), ch: 4 (over z_lo, core).
Axes of the slice: x: 4, y: 4, z: 4 (z_hi: 2, z_lo: 2; z = z_hi * 2 + z_lo), core: 2. Of those that a mesh axis runs over, the one named last changes fastest.
Arguments:
- signal: bfloat16 [128, 524288], P('ch', 'ctx'), parts along dimension 0, may hold values from -6 to 6
- filter_taps: float32 [128, 524288], P('ch', 'ctx'), parts along dimension 0, may hold values from -0.0078125 to 0.0078125
- gate_values: bfloat16 [128, 524288], P('ch', 'ctx'), parts along dimension 0, may hold values from -6 to 6
- skip_gain: float32 [128], P('ch'), parts along dimension 0, may hold values from -4 to 4
Outputs:
- gated_output: bfloat16 [128, 524288], P('ch', 'ctx'), parts along dimension 0
There are 4 independent parts, one for each index of `ch`. A program takes and returns all parts, laid end to end along the dimension named above; each array names one. Nothing has to cross between parts.
All inputs are finite; a program needn't handle non-finite values.
Results may differ from a plain program's by a relative error of at most 0.001.
Values sent between devices are 32-bit elements; how exact they have to be, the bound alone decides.
No kernel may reach another device: no remote copies, remote signals or barrier semaphores. Data moves between devices by JAX's collectives and lax.ppermute only.
A program may use at most 128 MiB of HBM per device.

v0:
```python
import math

import jax
import jax.numpy as jnp
import numpy as np
from jax import lax
from jax.experimental import pallas as pl
from jax.experimental.pallas import tpu as pltpu
from jax.sharding import PartitionSpec as P

F32 = jnp.float32
BF16 = jnp.bfloat16
ROWS = 256
MIDS = 16
LANES = 128
TOTAL = ROWS * MIDS * LANES


def wave(product, period):
    angle = 2.0 * np.pi * (product % period) / period
    return np.cos(angle), np.sin(angle)


def halves_of(table):
    upper = table.astype(jnp.bfloat16)
    lower = (table - upper.astype(np.float64)).astype(jnp.bfloat16)
    return upper, lower


def host_tables():
    n1 = np.arange(ROWS, dtype=np.int64)
    k1 = np.arange(ROWS, dtype=np.int64)
    cos1, sin1 = wave((4 * k1[:, None] + 1) * n1[None, :], 4 * ROWS)
    first = np.concatenate([cos1, -sin1], axis=0)
    lane = np.arange(LANES, dtype=np.int64)
    cos3, sin3 = wave(lane[:, None] * lane[None, :], LANES)
    third = np.block([[cos3, -sin3], [sin3, cos3]])
    k2 = np.arange(MIDS, dtype=np.int64)
    cos2, sin2 = wave(k2[:, None] * lane[None, :], MIDS * LANES)
    mid = np.stack([cos2, -sin2]).astype(np.float32)
    return first, third, mid


def row_twiddle():
    shape = (MIDS, ROWS, LANES)
    position = lax.broadcasted_iota(jnp.int32, shape, 0) * LANES + lax.broadcasted_iota(jnp.int32, shape, 2)
    product = position * (4 * lax.broadcasted_iota(jnp.int32, shape, 1) + 1)
    angle = (2.0 * math.pi / (4 * TOTAL)) * (product % (4 * TOTAL)).astype(F32)
    return jnp.cos(angle), -jnp.sin(angle)


def split(values):
    upper = values.astype(BF16)
    return upper, (values - upper.astype(F32)).astype(BF16)


def dot(left, right):
    return jnp.dot(left, right, preferred_element_type=F32)


def times(a, b):
    return a[0] * b[0] - a[1] * b[1], a[0] * b[1] + a[1] * b[0]


def conj_times(a, b):
    return a[0] * b[0] + a[1] * b[1], a[1] * b[0] - a[0] * b[1]


def four_point(v, sign):
    s0 = (v[0][0] + v[2][0], v[0][1] + v[2][1])
    d0 = (v[0][0] - v[2][0], v[0][1] - v[2][1])
    s1 = (v[1][0] + v[3][0], v[1][1] + v[3][1])
    d1 = (v[1][0] - v[3][0], v[1][1] - v[3][1])
    r1 = (-sign * d1[1], sign * d1[0]) if sign > 0 else (d1[1], -d1[0])
    return [
        (s0[0] + s1[0], s0[1] + s1[1]),
        (d0[0] + r1[0], d0[1] + r1[1]),
        (s0[0] - s1[0], s0[1] - s1[1]),
        (d0[0] - r1[0], d0[1] - r1[1]),
    ]


def turn(v, step, sign):
    step = step % 16
    if step == 0:
        return v
    root = math.sqrt(0.5)
    if step == 2:
        if sign < 0:
            return ((v[0] + v[1]) * root, (v[1] - v[0]) * root)
        return ((v[0] - v[1]) * root, (v[1] + v[0]) * root)
    if step == 4:
        return (v[1], -v[0]) if sign < 0 else (-v[1], v[0])
    c, s = math.cos(2 * math.pi * step / 16), sign * math.sin(2 * math.pi * step / 16)
    return (v[0] * c - v[1] * s, v[0] * s + v[1] * c)


def sixteen_point(v, sign):
    columns = [four_point([v[4 * p + q] for p in range(4)], sign) for q in range(4)]
    out = [None] * 16
    for r in range(4):
        row = four_point([turn(columns[q][r], q * r, sign) for q in range(4)], sign)
        for s in range(4):
            out[r + 4 * s] = row[s]
    return out


def pack_kernel(src_ref, out_ref):
    channels, length = src_ref.shape
    for group in range(channels // 8):
        for row in range(length // LANES):
            value = src_ref[pl.ds(8 * group, 8), pl.ds(row * LANES, LANES)].astype(F32)
            place = (row % MIDS) * (LANES // MIDS) + row // MIDS
            out_ref[pl.ds(8 * group * LANES + place, 8, stride=LANES), :] = value


def pack(values):
    channels, length = values.shape
    block = 16
    return pl.pallas_call(
        pack_kernel,
        grid=(channels // block,),
        in_specs=[pl.BlockSpec((block, length), lambda i: (i, 0))],
        out_specs=pl.BlockSpec((block * LANES, LANES), lambda i: (i, 0)),
        out_shape=jax.ShapeDtypeStruct((channels * LANES, LANES), F32),
        name="pack",
    )(values)


def forward_rows(src_ref, first_hi, first_lo, tw_re, tw_im, work_re, work_im, exact):
    def step(pair, carry):
        even = src_ref[:, 2 * pair].reshape(ROWS, LANES)
        odd = src_ref[:, 2 * pair + 1].reshape(ROWS, LANES)
        values = jnp.concatenate([even, odd], axis=1)
        if exact:
            upper = values.astype(BF16)
            out = dot(first_hi[...], upper) + dot(first_lo[...], upper)
        else:
            upper, lower = split(values)
            out = dot(first_hi[...], upper) + (dot(first_lo[...], upper) + dot(first_hi[...], lower))
        for side in range(2):
            lanes = slice(side * LANES, (side + 1) * LANES)
            mid = 2 * pair + side
            re, im = times((out[:ROWS, lanes], out[ROWS:, lanes]), (tw_re[mid], tw_im[mid]))
            work_re[mid] = re
            work_im[mid] = im
        return carry

    lax.fori_loop(0, MIDS // 2, step, 0)


def forward_mids(mid_ref, work_re, work_im):
    def step(group, carry):
        rows = pl.ds(pl.multiple_of(group * 8, 8), 8)
        out = sixteen_point([(work_re[m, rows], work_im[m, rows]) for m in range(MIDS)], -1)
        for k in range(MIDS):
            value = out[k]
            if k:
                value = times(value, (mid_ref[0, k : k + 1], mid_ref[1, k : k + 1]))
            work_re[k, rows] = value[0]
            work_im[k, rows] = value[1]
        return carry

    lax.fori_loop(0, ROWS // 8, step, 0)


def lane_stage(values, third_hi, third_lo):
    upper, lower = split(values)
    return dot(upper, third_hi[...]) + (dot(upper, third_lo[...]) + dot(lower, third_hi[...]))


def taps_kernel(src_ref, first_hi, first_lo, third_hi, third_lo, mid_ref, tw_re, tw_im, out_ref, work_re, work_im):
    forward_rows(src_ref, first_hi, first_lo, tw_re, tw_im, work_re, work_im, False)
    forward_mids(mid_ref, work_re, work_im)

    def step(k, carry):
        values = jnp.concatenate([work_re[k], work_im[k]], axis=1)
        out_ref[k] = lane_stage(values, third_hi, third_lo)
        return carry

    lax.fori_loop(0, MIDS, step, 0)


def signal_kernel(
    src_ref, spec_ref, first_hi, first_lo, back_hi, back_lo, third_hi, third_lo, undo_hi, undo_lo,
    mid_ref, tw_re, tw_im, out_ref, work_re, work_im,
):
    forward_rows(src_ref, first_hi, first_lo, tw_re, tw_im, work_re, work_im, True)
    forward_mids(mid_ref, work_re, work_im)

    def step(k, carry):
        values = jnp.concatenate([work_re[k], work_im[k]], axis=1)
        seen = lane_stage(values, third_hi, third_lo)
        spec = spec_ref[k]
        prod = times((seen[:, :LANES], seen[:, LANES:]), (spec[:, :LANES], spec[:, LANES:]))
        back = lane_stage(jnp.concatenate(prod, axis=1), undo_hi, undo_lo)
        work_re[k] = back[:, :LANES]
        work_im[k] = back[:, LANES:]
        return carry

    lax.fori_loop(0, MIDS, step, 0)

    def mids(group, carry):
        rows = pl.ds(pl.multiple_of(group * 8, 8), 8)
        values = []
        for k in range(MIDS):
            value = (work_re[k, rows], work_im[k, rows])
            if k:
                value = conj_times(value, (mid_ref[0, k : k + 1], mid_ref[1, k : k + 1]))
            values.append(value)
        out = sixteen_point(values, 1)
        for m in range(MIDS):
            re, im = conj_times(out[m], (tw_re[m, rows], tw_im[m, rows]))
            work_re[m, rows] = re
            work_im[m, rows] = im
        return carry

    lax.fori_loop(0, ROWS // 8, mids, 0)

    def last(pair, carry):
        values = jnp.concatenate(
            [
                jnp.concatenate([work_re[2 * pair], work_im[2 * pair]], axis=0),
                jnp.concatenate([work_re[2 * pair + 1], work_im[2 * pair + 1]], axis=0),
            ],
            axis=1,
        )
        upper, lower = split(values)
        out = dot(back_hi[...], upper) + (dot(back_lo[...], upper) + dot(back_hi[...], lower))
        blocks = src_ref.shape[0]
        out_ref[:, 2 * pair] = out[:, :LANES].reshape(blocks, ROWS // blocks, LANES)
        out_ref[:, 2 * pair + 1] = out[:, LANES:].reshape(blocks, ROWS // blocks, LANES)
        return carry

    lax.fori_loop(0, MIDS // 2, last, 0)


def gate_kernel(conv_ref, signal_ref, gate_ref, skip_ref, out_ref):
    channels, length = signal_ref.shape
    for group in range(channels // 8):
        skip = skip_ref[pl.ds(8 * group, 8), :]
        for row in range(length // LANES):
            where = (pl.ds(8 * group, 8), pl.ds(row * LANES, LANES))
            place = (row % MIDS) * (LANES // MIDS) + row // MIDS
            conv = conv_ref[pl.ds(8 * group * LANES + place, 8, stride=LANES), :]
            total = conv + skip * signal_ref[where].astype(F32)
            out_ref[where] = (gate_ref[where].astype(F32) * total).astype(BF16)


def gate(conv, signal, gate_values, skip_gain):
    channels, length = signal.shape
    block = 16
    skip = jnp.broadcast_to(skip_gain[:, None], (channels, LANES))
    line = pl.BlockSpec((block, length), lambda i: (i, 0))
    return pl.pallas_call(
        gate_kernel,
        grid=(channels // block,),
        in_specs=[
            pl.BlockSpec((block * LANES, LANES), lambda i: (i, 0)),
            line,
            line,
            pl.BlockSpec((block, LANES), lambda i: (i, 0)),
        ],
        out_specs=line,
        out_shape=jax.ShapeDtypeStruct((channels, length), BF16),
        name="gate",
    )(conv, signal, gate_values, skip)


def tables():
    first, third, mid = host_tables()
    first_hi, first_lo = halves_of(first)
    back_hi, back_lo = halves_of(first.T.copy())
    third_hi, third_lo = halves_of(third)
    undo_hi, undo_lo = halves_of(third.T.copy() / TOTAL)
    return dict(
        first=(first_hi, first_lo), back=(back_hi, back_lo), third=(third_hi, third_lo),
        undo=(undo_hi, undo_lo), mid=mid,
    )


def transform_taps(taps, tab, twiddle):
    return pl.pallas_call(
        taps_kernel,
        out_shape=jax.ShapeDtypeStruct((MIDS, ROWS, 2 * LANES), F32),
        scratch_shapes=[pltpu.VMEM((MIDS, ROWS, LANES), F32)] * 2,
        name="taps",
    )(taps, *tab["first"], *tab["third"], tab["mid"], *twiddle)


def convolve(values, spectrum, tab, twiddle):
    return pl.pallas_call(
        signal_kernel,
        out_shape=jax.ShapeDtypeStruct(values.shape, F32),
        scratch_shapes=[pltpu.VMEM((MIDS, ROWS, LANES), F32)] * 2,
        name="convolve",
    )(values, spectrum, *tab["first"], *tab["back"], *tab["third"], *tab["undo"], tab["mid"], *twiddle)


def shards(signal, filter_taps, gate_values, skip_gain):
    channels, length = signal.shape
    blocks = lax.axis_size("ctx")
    shape = (blocks, MIDS, ROWS // blocks, LANES)
    tab = {k: jax.tree.map(jnp.asarray, v) for k, v in tables().items()}

    def exchange(values):
        return lax.all_to_all(values.reshape(shape), "ctx", split_axis=0, concat_axis=0, tiled=True)

    taps = exchange(pack(filter_taps))
    values = exchange(pack(signal))
    twiddle = row_twiddle()
    spectrum = transform_taps(taps, tab, twiddle)
    conv = convolve(values, spectrum, tab, twiddle)
    back = exchange(conv).reshape(channels * LANES, LANES)
    return gate(back, signal, gate_values, skip_gain)


def solution(mesh):
    in_specs = (P("ch", "ctx"), P("ch", "ctx"), P("ch", "ctx"), P("ch"))
    out_specs = P("ch", "ctx")
    return jax.shard_map(shards, mesh=mesh, in_specs=in_specs, out_specs=out_specs, check_vma=False)
```

profile of v0, /device:TPU:1, one launch (start us, length us, event | category | flops | bytes accessed | tf_op | source)
XLA Modules:
  0.0 142.8 jit_solution(8338832449494930976)
XLA Ops:
  0.0 3.5 %pack.3 = f32[4096,128]{1,0:T(8,128)} custom-call(f32[32,16384]{1,0:T(8,128)} %src_ref.3), custom_call_target="tpu_custom_call" | custom-call | tf_op jit(solution)/shard_map/pack/pallas_call | solution.py:120
  3.5 11.2 %all-to-all-start.1 = ((f32[32,16,8,128]{3,2,1,0:T(8,128)}), f32[32,16,8,128]{3,2,1,0:T(8,128)S(1)}, u32[]{:S(2)}, u32[]{:S(2)}) async-start(f32[32,16,8,128]{3,2,1,0:T(8,128)} %bitcast.4), calls=%async_computation.1 | async-start | bytes 4194304 | tf_op jit(solution)/shard_map/all_to_all | solution.py:307
  14.7 3.3 %pack.2 = f32[4096,128]{1,0:T(8,128)} custom-call(bf16[32,16384]{1,0:T(8,128)(2,1)} %signal_ref.1), custom_call_target="tpu_custom_call" | custom-call | tf_op jit(solution)/shard_map/pack/pallas_call | solution.py:120
  18.0 25.2 %all-to-all-done.1.src_ref = f32[32,16,8,128]{3,2,1,0:T(8,128)S(1)} async-done(((f32[32,16,8,128]{3,2,1,0:T(8,128)}), f32[32,16,8,128]{3,2,1,0:T(8,128)S(1)}, u32[]{:S(2)}, u32[]{:S(2)}) %all-to-all-start.1) | async-done | bytes 2097184 | tf_op jit(solution)/shard_map/all_to_all | solution.py:307
  43.2 0.0 copy-start.1
  43.2 1.3 copy-done.1
  44.5 6.5 %all-to-all-start = ((f32[32,16,8,128]{3,2,1,0:T(8,128)}), f32[32,16,8,128]{3,2,1,0:T(8,128)S(1)}, u32[]{:S(2)}, u32[]{:S(2)}) async-start(f32[32,16,8,128]{3,2,1,0:T(8,128)} %bitcast.3), calls=%async_computation | async-start | bytes 4194304 | tf_op jit(solution)/shard_map/all_to_all | solution.py:307
  51.1 9.7 %sine_negate_fusion = (f32[16,256,128]{2,1,0:T(8,128)}, f32[16,256,128]{2,1,0:T(8,128)}) fusion(s32[256]{0:T(256)S(1)} %multiply_add_fusion, s32[16]{0:T(128)S(1)} %iota_multiply_fusion), kind=kLoop, calls=%fused_computation.6 | loop fusion | flops 8388608 | bytes 4195392 | tf_op jit(solution)/shard_map/neg | solution.py:49
  60.8 14.0 %taps.1.spec_ref = f32[16,256,256]{2,1,0:T(8,128)} custom-call(f32[32,16,8,128]{3,2,1,0:T(8,128)} %copy-done.1, bf16[512,256]{1,0:T(8,128)(2,1)} %constant.41.clone.first_hi, bf16[512,256]{1,0:T(8,128)(2,1)} %constant.42.clone.first_lo, bf16[256,256]{1,0:T(8,128)(2,1)} %constant.45.clone.third_hi, bf16[256,256]{1,0:T(8,128)(2,1)} %constant.46.clone.third_lo, ...), custom_call_target="tpu_custom_call" | custom-call | tf_op jit(solution)/shard_map/taps/pallas_call | solution.py:283
  74.8 3.8 %all-to-all-done.src_ref = f32[32,16,8,128]{3,2,1,0:T(8,128)S(1)} async-done(((f32[32,16,8,128]{3,2,1,0:T(8,128)}), f32[32,16,8,128]{3,2,1,0:T(8,128)S(1)}, u32[]{:S(2)}, u32[]{:S(2)}) %all-to-all-start) | async-done | bytes 2097184 | tf_op jit(solution)/shard_map/all_to_all | solution.py:307
  78.6 0.0 copy-start
  78.6 1.3 copy-done
  79.9 24.7 %convolve.1 = f32[32,16,8,128]{3,2,1,0:T(8,128)} custom-call(f32[32,16,8,128]{3,2,1,0:T(8,128)} %copy-done, f32[16,256,256]{2,1,0:T(8,128)} %taps.1.spec_ref, bf16[512,256]{1,0:T(8,128)(2,1)} %constant.41.clone.first_hi, bf16[512,256]{1,0:T(8,128)(2,1)} %constant.42.clone.first_lo, bf16[256,512]{1,0:T(8,128)(2,1)} %constant.43.clone.back_hi, ...), custom_call_target="tpu_custom_call" | custom-call | tf_op jit(solution)/shard_map/convolve/pallas_call | solution.py:292
  104.7 0.0 copy-start.2
  104.7 33.8 %all_to_all.15 = f32[32,16,8,128]{3,2,1,0:T(8,128)} all-to-all(f32[32,16,8,128]{3,2,1,0:T(8,128)} %convolve.1), channel_id=1, replica_groups=mesh['ctx'=32,'ch'=4] {'ctx'}, dimensions={0} | all-to-all | bytes 4194304 | tf_op jit(solution)/shard_map/all_to_all | solution.py:307
  138.5 0.0 copy-done.2
  138.5 0.7 broadcast_in_dim.2.skip_ref
  139.2 3.6 %gate.1 = bf16[32,16384]{1,0:T(8,128)(2,1)} custom-call(f32[4096,128]{1,0:T(8,128)} %bitcast.5, bf16[32,16384]{1,0:T(8,128)(2,1)} %signal_ref.1, bf16[32,16384]{1,0:T(8,128)(2,1)} %gate_ref.1, f32[32,128]{1,0:T(8,128)} %broadcast_in_dim.2.skip_ref), custom_call_target="tpu_custom_call" | custom-call | tf_op jit(solution)/shard_map/gate/pallas_call | solution.py:255
  (2 shorter events, 0.0 us)
Async XLA Ops:
  3.5 39.7 %all-to-all-start.1 = ((f32[32,16,8,128]{3,2,1,0:T(8,128)}), f32[32,16,8,128]{3,2,1,0:T(8,128)S(1)}, u32[]{:S(2)}, u32[]{:S(2)}) async-start(f32[32,16,8,128]{3,2,1,0:T(8,128)} %bitcast.4), calls=%async_computation.1 | async-start | bytes 4194304 | tf_op jit(solution)/shard_map/all_to_all | solution.py:307
  43.2 1.3 copy-start.1
  44.5 34.1 %all-to-all-start = ((f32[32,16,8,128]{3,2,1,0:T(8,128)}), f32[32,16,8,128]{3,2,1,0:T(8,128)S(1)}, u32[]{:S(2)}, u32[]{:S(2)}) async-start(f32[32,16,8,128]{3,2,1,0:T(8,128)} %bitcast.3), calls=%async_computation | async-start | bytes 4194304 | tf_op jit(solution)/shard_map/all_to_all | solution.py:307
  78.6 1.3 copy-start
  104.7 33.8 %copy-start.2 = (f32[32]{0:T(128)S(1)}, f32[32]{0:T(128)}, u32[]{:S(2)}) copy-start(f32[32]{0:T(128)} %param.16) | copy-start | bytes 388
where the time goes:
time: 145 us; the launch traced here: 143 us
  Pallas kernels  49.1 us (34%)
  blocking collectives  33.8 us (23%)
  waiting for transfers between devices  29 us (20%)
  starting transfers between devices  17.7 us (12%)
  other arithmetic  9.75 us (7%)
  local copies, waits for them, and re-layouts  3.33 us (2%)
    all_to_all x1, blocking collectives, exchange(): lax.all_to_all(values.reshape(shape), 'ctx', split_axis=0, concat_axis=0,...  33.8 us
    all_to_all x2, waiting for transfers between devices, exchange(): lax.all_to_all(values.reshape(shape), 'ctx', split_axis=0, concat_axis=0,...  29 us
    pallas_call x1, Pallas kernels, convolve(): pl.pallas_call(signal_kernel, out_shape=jax.ShapeDtypeStruct(values.shape...  24.7 us
    all_to_all x2, starting transfers between devices, exchange(): lax.all_to_all(values.reshape(shape), 'ctx', split_axis=0, concat_axis=0,...  17.7 us
    pallas_call x1, Pallas kernels, transform_taps(): pl.pallas_call(taps_kernel, out_shape=jax.ShapeDtypeStruct((MIDS, ROWS, 2...  14 us
    neg x1, other arithmetic, row_twiddle(): return (jnp.cos(angle), -jnp.sin(angle))  9.74 us
    pallas_call x2, Pallas kernels, pack(): pl.pallas_call(pack_kernel, grid=(channels // block,), in_specs=[pl.Block...  6.78 us
    pallas_call x1, Pallas kernels, gate(): pl.pallas_call(gate_kernel, grid=(channels // block,), in_specs=[pl.Block...  3.6 us
  transfers between devices with their start and end apart: 2, of which 2 were waited for; matrix products, arithmetic and copies ran while one was open for 7% of the time, Pallas kernels for 12%

commit v1 on v0

v1 whole, which is shorter than its diff:
```python
import math

import jax
import jax.numpy as jnp
import numpy as np
from jax import lax
from jax.experimental import pallas as pl
from jax.experimental.pallas import tpu as pltpu
from jax.sharding import PartitionSpec as P

F32 = jnp.float32
BF16 = jnp.bfloat16
ROWS = 256
MIDS = 16
LANES = 128
TOTAL = ROWS * MIDS * LANES


def wave(product, period):
    angle = 2.0 * np.pi * (product % period) / period
    return np.cos(angle), np.sin(angle)


def halves_of(table):
    upper = table.astype(jnp.bfloat16)
    lower = (table - upper.astype(np.float64)).astype(jnp.bfloat16)
    return upper, lower


def host_tables():
    n1 = np.arange(ROWS, dtype=np.int64)
    k1 = np.arange(ROWS, dtype=np.int64)
    cos1, sin1 = wave((4 * k1[:, None] + 1) * n1[None, :], 4 * ROWS)
    first = np.concatenate([cos1, -sin1], axis=0)
    lane = np.arange(LANES, dtype=np.int64)
    cos3, sin3 = wave(lane[:, None] * lane[None, :], LANES)
    third = np.block([[cos3, -sin3], [sin3, cos3]])
    k2 = np.arange(MIDS, dtype=np.int64)
    cos2, sin2 = wave(k2[:, None] * lane[None, :], MIDS * LANES)
    mid = np.stack([cos2, -sin2]).astype(np.float32)
    cosp, sinp = wave((4 * k1[:, None] + 1) * lane[None, :], 4 * TOTAL)
    cose, sine = wave(np.broadcast_to((4 * k1[:, None] + 1) * LANES, (ROWS, LANES)), 4 * TOTAL)
    twist = np.stack([cosp, -sinp, cose, -sine]).astype(np.float32)
    return first, third, mid, twist


def split(values):
    upper = values.astype(BF16)
    return upper, (values - upper.astype(F32)).astype(BF16)


def dot(left, right):
    return jnp.dot(left, right, preferred_element_type=F32)


def times(a, b):
    return a[0] * b[0] - a[1] * b[1], a[0] * b[1] + a[1] * b[0]


def conj_times(a, b):
    return a[0] * b[0] + a[1] * b[1], a[1] * b[0] - a[0] * b[1]


def four_point(v, sign):
    s0 = (v[0][0] + v[2][0], v[0][1] + v[2][1])
    d0 = (v[0][0] - v[2][0], v[0][1] - v[2][1])
    s1 = (v[1][0] + v[3][0], v[1][1] + v[3][1])
    d1 = (v[1][0] - v[3][0], v[1][1] - v[3][1])
    r1 = (-sign * d1[1], sign * d1[0]) if sign > 0 else (d1[1], -d1[0])
    return [
        (s0[0] + s1[0], s0[1] + s1[1]),
        (d0[0] + r1[0], d0[1] + r1[1]),
        (s0[0] - s1[0], s0[1] - s1[1]),
        (d0[0] - r1[0], d0[1] - r1[1]),
    ]


def turn(v, step, sign):
    step = step % 16
    if step == 0:
        return v
    root = math.sqrt(0.5)
    if step == 2:
        if sign < 0:
            return ((v[0] + v[1]) * root, (v[1] - v[0]) * root)
        return ((v[0] - v[1]) * root, (v[1] + v[0]) * root)
    if step == 4:
        return (v[1], -v[0]) if sign < 0 else (-v[1], v[0])
    c, s = math.cos(2 * math.pi * step / 16), sign * math.sin(2 * math.pi * step / 16)
    return (v[0] * c - v[1] * s, v[0] * s + v[1] * c)


def sixteen_point(v, sign):
    columns = [four_point([v[4 * p + q] for p in range(4)], sign) for q in range(4)]
    out = [None] * 16
    for r in range(4):
        row = four_point([turn(columns[q][r], q * r, sign) for q in range(4)], sign)
        for s in range(4):
            out[r + 4 * s] = row[s]
    return out


NEAR = LANES // MIDS
BLOCK = 64
HBM = pl.BlockSpec(memory_space=pltpu.HBM)
ANY = pl.BlockSpec(memory_space=pl.ANY)


def tile_view(values):
    channels, length = values.shape
    return values.reshape(channels // 8, 8, length // LANES, LANES).transpose(0, 2, 1, 3)


def send_chunks(buf, out_ref, sems, group):
    copies = [
        pltpu.make_async_copy(buf.at[group, :, c, :], out_ref.at[8 * group + c], sems.at[8 * group + c])
        for c in range(8)
    ]
    for copy in copies:
        copy.start()
    return copies


def pack_taps_kernel(src_ref, out_ref, buf, in_sems, out_sems):
    groups = src_ref.shape[0]
    loads = [pltpu.make_async_copy(src_ref.at[g], buf.at[g], in_sems.at[g]) for g in range(groups)]
    for load in loads:
        load.start()
    sends = []
    for g in range(groups):
        loads[g].wait()
        sends += send_chunks(buf, out_ref, out_sems, g)
    for send in sends:
        send.wait()


def pack_taps(values):
    channels, length = values.shape
    view = tile_view(values)
    return pl.pallas_call(
        pack_taps_kernel,
        in_specs=[HBM],
        out_specs=HBM,
        out_shape=jax.ShapeDtypeStruct((channels, length // LANES, LANES), F32),
        scratch_shapes=[
            pltpu.VMEM(view.shape, F32),
            pltpu.SemaphoreType.DMA((channels // 8,)),
            pltpu.SemaphoreType.DMA((channels,)),
        ],
        name="pack_taps",
    )(view)


def pack_kernel(src_ref, out_ref):
    channels, length = src_ref.shape
    rows = length // LANES
    for group in range(channels // 8):
        for row in range(rows):
            value = src_ref[pl.ds(8 * group, 8), pl.ds(row * LANES, LANES)].astype(F32)
            out_ref[pl.ds(8 * group * rows + row, 8, stride=rows), :] = value


def pack(values):
    channels, length = values.shape
    block = 16
    rows = length // LANES
    return pl.pallas_call(
        pack_kernel,
        grid=(channels // block,),
        in_specs=[pl.BlockSpec((block, length), lambda i: (i, 0))],
        out_specs=pl.BlockSpec((block * rows, LANES), lambda i: (i, 0)),
        out_shape=jax.ShapeDtypeStruct((channels * rows, LANES), F32),
        name="pack",
    )(values)


def gate_kernel(conv_ref, signal_ref, gate_ref, skip_ref, out_ref, buf, out, sems, out_sems):
    groups, rows = buf.shape[:2]
    loads = [
        pltpu.make_async_copy(conv_ref.at[8 * g + c], buf.at[g, :, c, :], sems.at[8 * g + c])
        for g in range(groups)
        for c in range(8)
    ]
    for load in loads:
        load.start()
    stores = []
    for g in range(groups):
        lines = pl.ds(8 * g, 8)
        skip = skip_ref[lines, :]
        for c in range(8):
            loads[8 * g + c].wait()
        for row in range(rows):
            where = (lines, pl.ds(row * LANES, LANES))
            total = buf[g, row] + skip * signal_ref[where].astype(F32)
            out[where] = (gate_ref[where].astype(F32) * total).astype(BF16)
        if g % 2:
            pair = pl.ds(8 * g - 8, 16)
            stores.append(pltpu.make_async_copy(out.at[pair, :], out_ref.at[pair, :], out_sems.at[g // 2]))
            stores[-1].start()
    for store in stores:
        store.wait()


def gate(conv, signal, gate_values, skip):
    channels, length = signal.shape
    rows = length // LANES
    vmem = pl.BlockSpec(memory_space=pltpu.VMEM)
    return pl.pallas_call(
        gate_kernel,
        in_specs=[ANY, vmem, vmem, vmem],
        out_specs=HBM,
        out_shape=jax.ShapeDtypeStruct((channels, length), BF16),
        scratch_shapes=[
            pltpu.VMEM((channels // 8, rows, 8, LANES), F32),
            pltpu.VMEM((channels, length), BF16),
            pltpu.SemaphoreType.DMA((channels,)),
            pltpu.SemaphoreType.DMA((channels // 16,)),
        ],
        compiler_params=pltpu.CompilerParams(vmem_limit_bytes=16 << 20),
        name="gate",
    )(conv, signal, gate_values, skip)


def forward_rows(src, loads, first_hi, first_lo, twist, turn_re, turn_im, work_re, work_im, exact):
    turn_re[...] = twist[0]
    turn_im[...] = twist[1]

    def step(pair, carry):
        for side in range(2):
            loads(2 * pair + side).wait()
        values = jnp.concatenate([src[2 * pair].reshape(ROWS, LANES), src[2 * pair + 1].reshape(ROWS, LANES)], axis=1)
        if exact:
            upper = values.astype(BF16)
            out = dot(first_hi[...], upper) + dot(first_lo[...], upper)
        else:
            upper, lower = split(values)
            out = dot(first_hi[...], upper) + (dot(first_lo[...], upper) + dot(first_hi[...], lower))
        turned = (turn_re[...], turn_im[...])
        for side in range(2):
            lanes = slice(side * LANES, (side + 1) * LANES)
            re, im = times((out[:ROWS, lanes], out[ROWS:, lanes]), turned)
            work_re[2 * pair + side] = re
            work_im[2 * pair + side] = im
            turned = times(turned, (twist[2], twist[3]))
        turn_re[...] = turned[0]
        turn_im[...] = turned[1]
        return carry

    lax.fori_loop(0, MIDS // 2, step, 0)


def forward_mids(mid_ref, work_re, work_im, base, out_re, out_im, place):
    rows, to = pl.ds(base, 8), pl.ds(place, 8)
    out = sixteen_point([(work_re[m, rows], work_im[m, rows]) for m in range(MIDS)], -1)
    for k in range(MIDS):
        value = out[k]
        if k:
            value = times(value, (mid_ref[0, k : k + 1], mid_ref[1, k : k + 1]))
        out_re[k, to] = value[0]
        out_im[k, to] = value[1]


def inverse_mids(mid_ref, twist, work_re, work_im, place, out_re, out_im, base):
    rows, to = pl.ds(place, 8), pl.ds(base, 8)
    values = []
    for k in range(MIDS):
        value = (work_re[k, rows], work_im[k, rows])
        if k:
            value = conj_times(value, (mid_ref[0, k : k + 1], mid_ref[1, k : k + 1]))
        values.append(value)
    out = sixteen_point(values, 1)
    turned = (twist[0, to], twist[1, to])
    step = (twist[2, to], twist[3, to])
    for m in range(MIDS):
        re, im = conj_times(out[m], turned)
        out_re[m, to] = re
        out_im[m, to] = im
        if m + 1 < MIDS:
            turned = times(turned, step)


def lane_stage(values, third_hi, third_lo):
    upper, lower = split(values)
    rows = values.shape[0]
    both = dot(jnp.concatenate([upper, lower], axis=0), third_hi[...])
    return both[:rows] + (both[rows:] + dot(upper, third_lo[...]))


def column(src_ref, buf, sems):
    return lambda m: pltpu.make_async_copy(src_ref.at[:, :, m, :], buf.at[m], sems.at[m])


def taps_kernel(
    src_ref, first_hi, first_lo, third_hi, third_lo, mid_ref, twist, out_ref,
    src, turn_re, turn_im, work_re, work_im, sems,
):
    loads = column(src_ref, src, sems)
    for m in range(MIDS):
        loads(m).start()
    forward_rows(src, loads, first_hi, first_lo, twist, turn_re, turn_im, work_re, work_im, False)

    def mids(group, carry):
        base = pl.multiple_of(group * 8, 8)
        forward_mids(mid_ref, work_re, work_im, base, work_re, work_im, base)
        return carry

    lax.fori_loop(0, ROWS // 8, mids, 0)

    def step(k, carry):
        values = jnp.concatenate([work_re[k], work_im[k]], axis=1)
        out_ref[k] = lane_stage(values, third_hi, third_lo)
        return carry

    lax.fori_loop(0, MIDS, step, 0)


SMALL = ("first_hi", "first_lo", "back", "back_hi", "third_hi", "third_lo", "undo_hi", "undo_lo", "mid", "twist")


def convolve_kernel(src_ref, spec_ref, *refs):
    count = len(SMALL)
    tables, out_ref, scratch = refs[:count], refs[count], refs[count + 1 :]
    local, (src, spec, out, turn_re, turn_im, work_re, work_im, done_re, done_im) = scratch[:count], scratch[count : count + 9]
    blocks = [scratch[count + 9 + 4 * i : count + 13 + 4 * i] for i in range(2)]
    sems, table_sems, spec_sem, out_sems = scratch[count + 17 :]
    tab = dict(zip(SMALL, local))
    loads = column(src_ref, src, sems)
    table_loads = {
        name: pltpu.make_async_copy(tables[i], local[i], table_sems.at[i]) for i, name in enumerate(SMALL)
    }
    spec_load = pltpu.make_async_copy(spec_ref, spec, spec_sem)
    early = ("first_hi", "first_lo", "twist")
    for name in early:
        table_loads[name].start()
    for m in range(MIDS):
        loads(m).start()
    for name in SMALL:
        if name not in early:
            table_loads[name].start()
    spec_load.start()
    for name in early:
        table_loads[name].wait()
    forward_rows(src, loads, tab["first_hi"], tab["first_lo"], tab["twist"], turn_re, turn_im, work_re, work_im, True)
    for name in SMALL:
        if name not in early:
            table_loads[name].wait()
    spec_load.wait()
    mid, twist = tab["mid"], tab["twist"]

    def forward(j):
        for g in range(BLOCK // 8):
            forward_mids(mid, work_re, work_im, j * BLOCK + 8 * g, blocks[j % 2][0], blocks[j % 2][1], 8 * g)

    def backward(j):
        for g in range(BLOCK // 8):
            inverse_mids(mid, twist, blocks[j % 2][2], blocks[j % 2][3], 8 * g, done_re, done_im, j * BLOCK + 8 * g)

    def lanes(j):
        in_re, in_im, out_re, out_im = blocks[j % 2]
        rows = MIDS * BLOCK
        values = jnp.concatenate([in_re[...].reshape(rows, LANES), in_im[...].reshape(rows, LANES)], axis=1)
        seen = lane_stage(values, tab["third_hi"], tab["third_lo"])
        wave_h = spec[:, pl.ds(j * BLOCK, BLOCK), :].reshape(rows, 2 * LANES)
        prod = times((seen[:, :LANES], seen[:, LANES:]), (wave_h[:, :LANES], wave_h[:, LANES:]))
        back = lane_stage(jnp.concatenate(prod, axis=1), tab["undo_hi"], tab["undo_lo"])
        out_re[...] = back[:, :LANES].reshape(MIDS, BLOCK, LANES)
        out_im[...] = back[:, LANES:].reshape(MIDS, BLOCK, LANES)

    steps = ROWS // BLOCK
    forward(0)
    for j in range(steps):
        lanes(j)
        if j + 1 < steps:
            forward(j + 1)
        if j:
            backward(j - 1)
    backward(steps - 1)

    def store(m):
        return pltpu.make_async_copy(out.at[m], out_ref.at[:, :, m, :], out_sems.at[m])

    def last(pair, carry):
        values = jnp.concatenate(
            [
                jnp.concatenate([done_re[2 * pair], done_im[2 * pair]], axis=0),
                jnp.concatenate([done_re[2 * pair + 1], done_im[2 * pair + 1]], axis=0),
            ],
            axis=1,
        )
        upper, lower = split(values)
        both = dot(tab["back"][...], upper)
        result = both[:ROWS] + (both[ROWS:] + dot(tab["back_hi"][...], lower))
        for side in range(2):
            out[2 * pair + side] = result[:, side * LANES : (side + 1) * LANES].reshape(out.shape[1:])
            store(2 * pair + side).start()
        return carry

    lax.fori_loop(0, MIDS // 2, last, 0)
    for m in range(MIDS):
        store(m).wait()


def tables():
    first, third, mid, twist = host_tables()
    first_hi, first_lo = halves_of(first)
    back_hi, back_lo = halves_of(first.T.copy())
    third_hi, third_lo = halves_of(third)
    undo_hi, undo_lo = halves_of(third.T.copy() / TOTAL)
    return dict(
        first_hi=first_hi, first_lo=first_lo, back=np.concatenate([back_hi, back_lo], axis=0), back_hi=back_hi,
        third_hi=third_hi, third_lo=third_lo, undo_hi=undo_hi, undo_lo=undo_lo, mid=mid, twist=twist,
    )


def column_scratch(blocks):
    return pltpu.VMEM((MIDS, blocks, ROWS // blocks, LANES), F32)


def transform_taps(taps, tab):
    names = ("first_hi", "first_lo", "third_hi", "third_lo", "mid", "twist")
    vmem = pl.BlockSpec(memory_space=pltpu.VMEM)
    return pl.pallas_call(
        taps_kernel,
        in_specs=[vmem] + [vmem] * len(names),
        out_shape=jax.ShapeDtypeStruct((MIDS, ROWS, 2 * LANES), F32),
        scratch_shapes=[column_scratch(taps.shape[0])]
        + [pltpu.VMEM((ROWS, LANES), F32)] * 2
        + [pltpu.VMEM((MIDS, ROWS, LANES), F32)] * 2
        + [pltpu.SemaphoreType.DMA((MIDS,))],
        compiler_params=pltpu.CompilerParams(vmem_limit_bytes=52 << 20),
        name="taps",
    )(taps, *(tab[n] for n in names))


def convolve(values, spectrum, tab):
    small = [tab[n] for n in SMALL]
    column_buf = column_scratch(values.shape[0])
    whole = pltpu.VMEM((MIDS, ROWS, LANES), F32)
    part = pltpu.VMEM((MIDS, BLOCK, LANES), F32)
    return pl.pallas_call(
        convolve_kernel,
        in_specs=[ANY] + [HBM] * (1 + len(small)),
        out_specs=HBM,
        out_shape=jax.ShapeDtypeStruct(values.shape, F32),
        scratch_shapes=[pltpu.VMEM(t.shape, t.dtype) for t in small]
        + [column_buf, pltpu.VMEM(spectrum.shape, F32), column_buf]
        + [pltpu.VMEM((ROWS, LANES), F32)] * 2
        + [whole] * 4
        + [part] * 8
        + [
            pltpu.SemaphoreType.DMA((MIDS,)),
            pltpu.SemaphoreType.DMA((len(small),)),
            pltpu.SemaphoreType.DMA(()),
            pltpu.SemaphoreType.DMA((MIDS,)),
        ],
        compiler_params=pltpu.CompilerParams(vmem_limit_bytes=58 << 20),
        name="convolve",
    )(values, spectrum, *small)


def shards(signal, filter_taps, gate_values, skip_gain):
    channels, length = signal.shape
    blocks = lax.axis_size("ctx")
    shape = (blocks, ROWS // blocks, MIDS, LANES)
    tab = {k: jnp.asarray(v) for k, v in tables().items()}

    def exchange(values):
        return lax.all_to_all(values.reshape(shape), "ctx", split_axis=0, concat_axis=0, tiled=True)

    taps = pltpu.with_memory_space_constraint(exchange(pack_taps(filter_taps)), pltpu.VMEM)
    skip = jnp.broadcast_to(skip_gain[:, None], (channels, LANES))
    packed, skip = lax.optimization_barrier((pack(signal), skip))
    values = exchange(packed)
    spectrum = transform_taps(taps, tab)
    conv = convolve(values, spectrum, tab)
    back = exchange(conv).reshape(channels, length // LANES, LANES)
    return gate(back, signal, gate_values, skip)


def solution(mesh):
    in_specs = (P("ch", "ctx"), P("ch", "ctx"), P("ch", "ctx"), P("ch"))
    out_specs = P("ch", "ctx")
    return jax.shard_map(shards, mesh=mesh, in_specs=in_specs, out_specs=out_specs, check_vma=False)
```

time: 145 us -> 131 us (0.903)
  Pallas kernels: 49.1 us -> 37.9 us
  waiting for transfers between devices: 29 us -> 38.9 us
  other arithmetic: 9.75 us -> 0 us
  local copies, waits for them, and re-layouts: 3.33 us -> 0.09 us
    all_to_all x2, waiting for transfers between devices: 29 us -> 38.9 us  [exchange(): lax.all_to_all(values.reshape(shape), 'ctx', split_axis=0, concat_axis=0,...]
    neg x1 -> x0, other arithmetic: 9.74 us -> none  [row_twiddle(): return (jnp.cos(angle), -jnp.sin(angle))]
    pallas_call x3 -> x4, Pallas kernels: 42.3 us -> 34.6 us  [the longest x1 15.1 us: convolve(): pl.pallas_call(convolve_kernel, in_specs=[ANY] + [HBM] * (1 + len(small))...]
    pallas_call x2 -> x1, Pallas kernels: 6.78 us -> 3.26 us  [pack(): pl.pallas_call(pack_kernel, grid=(channels // block,), in_specs=[pl.Block...]
    unnamed x6, local copies, waits for them, and re-layouts: 2.66 us -> 0.02 us
  transfers between devices with their start and end apart: 2 -> 2, of which waited for: 2 -> 2; matrix products, arithmetic and copies ran while one was open for 7% -> 0% of each run, Pallas kernels for 12% -> 13%
where the time goes in v1:
time: 131 us; the launch traced here: 129 us
  waiting for transfers between devices  38.9 us (30%)
  Pallas kernels  37.9 us (29%)
  blocking collectives  33.7 us (26%)
  starting transfers between devices  17.8 us (14%)
    all_to_all x2, waiting for transfers between devices, exchange(): lax.all_to_all(values.reshape(shape), 'ctx', split_axis=0, concat_axis=0,...  38.9 us
    all_to_all x1, blocking collectives, exchange(): lax.all_to_all(values.reshape(shape), 'ctx', split_axis=0, concat_axis=0,...  33.7 us
    all_to_all x2, starting transfers between devices, exchange(): lax.all_to_all(values.reshape(shape), 'ctx', split_axis=0, concat_axis=0,...  17.8 us
    pallas_call x1, Pallas kernels, convolve(): pl.pallas_call(convolve_kernel, in_specs=[ANY] + [HBM] * (1 + len(small))...  15.1 us
    pallas_call x1, Pallas kernels, transform_taps(): pl.pallas_call(taps_kernel, in_specs=[vmem] + [vmem] * len(names), out_sh...  13.8 us
    pallas_call x1, Pallas kernels, pack(): pl.pallas_call(pack_kernel, grid=(channels // block,), in_specs=[pl.Block...  3.26 us
    pallas_call x1, Pallas kernels, gate(): pl.pallas_call(gate_kernel, in_specs=[ANY, vmem, vmem, vmem], out_specs=H...  3.02 us
    pallas_call x1, Pallas kernels, pack_taps(): pl.pallas_call(pack_taps_kernel, in_specs=[HBM], out_specs=HBM, out_shape...  2.71 us
  transfers between devices with their start and end apart: 2, of which 2 were waited for; matrix products, arithmetic and copies ran while one was open for 0% of the time, Pallas kernels for 13%

profile of v1, /device:TPU:1, one launch (start us, length us, event | category | flops | bytes accessed | tf_op | source)
XLA Modules:
  0.0 128.5 jit_solution(5759397036869066517)
XLA Ops:
  0.0 2.7 %pack_taps.1 = f32[32,128,128]{2,1,0:T(8,128)} custom-call(f32[4,128,8,128]{3,2,1,0:T(8,128)} %bitcast.9), custom_call_target="tpu_custom_call" | custom-call | tf_op jit(solution)/shard_map/pack_taps/pallas_call | solution.py:140
  2.7 11.2 %all-to-all-start.1 = ((f32[32,8,16,128]{3,2,1,0:T(8,128)}), f32[32,8,16,128]{3,2,1,0:T(8,128)S(1)}, u32[]{:S(2)}, u32[]{:S(2)}) async-start(f32[32,8,16,128]{3,2,1,0:T(8,128)} %bitcast.8), calls=%async_computation.1 | async-start | bytes 4194304 | tf_op jit(solution)/shard_map/all_to_all | solution.py:468
  13.9 0.0 copy-start.2
  13.9 3.3 %pack.1 = f32[4096,128]{1,0:T(8,128)} custom-call(bf16[32,16384]{1,0:T(8,128)(2,1)} %signal_ref.1), custom_call_target="tpu_custom_call" | custom-call | tf_op jit(solution)/shard_map/pack/pallas_call | solution.py:167
  17.2 0.0 copy-done.2
  17.2 0.1 broadcast_in_dim.2.skip_ref
  17.3 25.1 %all-to-all-done.1.src_ref = f32[32,8,16,128]{3,2,1,0:T(8,128)S(1)} async-done(((f32[32,8,16,128]{3,2,1,0:T(8,128)}), f32[32,8,16,128]{3,2,1,0:T(8,128)S(1)}, u32[]{:S(2)}, u32[]{:S(2)}) %all-to-all-start.1) | async-done | bytes 2097184 | tf_op jit(solution)/shard_map/all_to_all | solution.py:468
  42.4 6.7 %all-to-all-start = ((f32[32,8,16,128]{3,2,1,0:T(8,128)}), f32[32,8,16,128]{3,2,1,0:T(8,128)}, u32[]{:S(2)}, u32[]{:S(2)}) async-start(f32[32,8,16,128]{3,2,1,0:T(8,128)} %bitcast.7), calls=%async_computation | async-start | bytes 4194304 | tf_op jit(solution)/shard_map/all_to_all | solution.py:468
  49.1 13.8 %taps.1.spec_ref = f32[16,256,256]{2,1,0:T(8,128)} custom-call(f32[32,8,16,128]{3,2,1,0:T(8,128)S(1)} %all-to-all-done.1.src_ref, bf16[512,256]{1,0:T(8,128)(2,1)} %constant.20.clone.first_hi.refs_0_, bf16[512,256]{1,0:T(8,128)(2,1)} %constant.21.clone.first_lo.refs_1_, bf16[256,256]{1,0:T(8,128)(2,1)} %constant.24.clone.third_hi.refs_4_, ...), custom_call_target="tpu_custom_call" | custom-call | tf_op jit(solution)/shard_map/taps/pallas_call | solution.py:422
  62.8 13.8 %all-to-all-done.src_ref = f32[32,8,16,128]{3,2,1,0:T(8,128)} async-done(((f32[32,8,16,128]{3,2,1,0:T(8,128)}), f32[32,8,16,128]{3,2,1,0:T(8,128)}, u32[]{:S(2)}, u32[]{:S(2)}) %all-to-all-start) | async-done | bytes 2097184 | tf_op jit(solution)/shard_map/all_to_all | solution.py:468
  76.6 15.1 %convolve.1 = f32[32,8,16,128]{3,2,1,0:T(8,128)} custom-call(f32[32,8,16,128]{3,2,1,0:T(8,128)} %all-to-all-done.src_ref, f32[16,256,256]{2,1,0:T(8,128)} %taps.1.spec_ref, bf16[512,256]{1,0:T(8,128)(2,1)} %constant.20.clone.first_hi.refs_0_, bf16[512,256]{1,0:T(8,128)(2,1)} %constant.21.clone.first_lo.refs_1_, bf16[512,512]{1,0:T(8,128)(2,1)} %constant.22.clone.refs_2_, ...), custom_call_target="tpu_custom_call" | custom-call | tf_op jit(solution)/shard_map/convolve/pallas_call | solution.py:440
  91.8 0.0 copy-start
  91.8 0.0 copy-start.1
  91.8 33.7 %all_to_all.15 = f32[32,8,16,128]{3,2,1,0:T(8,128)S(1)} all-to-all(f32[32,8,16,128]{3,2,1,0:T(8,128)} %convolve.1), channel_id=1, replica_groups=mesh['ctx'=32,'ch'=4] {'ctx'}, dimensions={0} | all-to-all | bytes 4194304 | tf_op jit(solution)/shard_map/all_to_all | solution.py:468
  125.5 0.0 copy-done
  125.5 0.0 copy-done.1
  125.5 3.0 %gate.1 = bf16[32,16384]{1,0:T(8,128)(2,1)} custom-call(f32[32,128,128]{2,1,0:T(8,128)S(1)} %bitcast.6, bf16[32,16384]{1,0:T(8,128)(2,1)S(1)} %copy-done, bf16[32,16384]{1,0:T(8,128)(2,1)S(1)} %copy-done.1, f32[32,128]{1,0:T(8,128)S(1)} %broadcast_in_dim.2.skip_ref), custom_call_target="tpu_custom_call" | custom-call | tf_op jit(solution)/shard_map/gate/pallas_call | solution.py:208
Async XLA Ops:
  2.7 39.7 %all-to-all-start.1 = ((f32[32,8,16,128]{3,2,1,0:T(8,128)}), f32[32,8,16,128]{3,2,1,0:T(8,128)S(1)}, u32[]{:S(2)}, u32[]{:S(2)}) async-start(f32[32,8,16,128]{3,2,1,0:T(8,128)} %bitcast.8), calls=%async_computation.1 | async-start | bytes 4194304 | tf_op jit(solution)/shard_map/all_to_all | solution.py:468
  13.9 3.3 %copy-start.2 = (f32[32]{0:T(128)S(1)}, f32[32]{0:T(128)}, u32[]{:S(2)}) copy-start(f32[32]{0:T(128)} %param.17) | copy-start | bytes 388
  42.4 34.2 %all-to-all-start = ((f32[32,8,16,128]{3,2,1,0:T(8,128)}), f32[32,8,16,128]{3,2,1,0:T(8,128)}, u32[]{:S(2)}, u32[]{:S(2)}) async-start(f32[32,8,16,128]{3,2,1,0:T(8,128)} %bitcast.7), calls=%async_computation | async-start | bytes 4194304 | tf_op jit(solution)/shard_map/all_to_all | solution.py:468
  91.8 33.8 %copy-start = (bf16[32,16384]{1,0:T(8,128)(2,1)S(1)}, bf16[32,16384]{1,0:T(8,128)(2,1)}, u32[]{:S(2)}) copy-start(bf16[32,16384]{1,0:T(8,128)(2,1)} %signal_ref.1) | copy-start | bytes 3145732
  91.8 33.7 %copy-start.1 = (bf16[32,16384]{1,0:T(8,128)(2,1)S(1)}, bf16[32,16384]{1,0:T(8,128)(2,1)}, u32[]{:S(2)}) copy-start(bf16[32,16384]{1,0:T(8,128)(2,1)} %gate_ref.1) | copy-start | bytes 3145732

commit v2 on v1

--- a/solution.py
+++ b/solution.py
@@ -101,6 +101,7 @@
 
 
 NEAR = LANES // MIDS
+STAGGER_NS = 15000
 BLOCK = 64
 HBM = pl.BlockSpec(memory_space=pltpu.HBM)
 ANY = pl.BlockSpec(memory_space=pl.ANY)
@@ -121,8 +122,13 @@
     return copies
 
 
-def pack_taps_kernel(src_ref, out_ref, buf, in_sems, out_sems):
+def pack_taps_kernel(late_ref, src_ref, out_ref, buf, in_sems, out_sems):
     groups = src_ref.shape[0]
+
+    @pl.when(late_ref[0] == 1)
+    def _():
+        pl.delay(STAGGER_NS)
+
     loads = [pltpu.make_async_copy(src_ref.at[g], buf.at[g], in_sems.at[g]) for g in range(groups)]
     for load in loads:
         load.start()
@@ -134,12 +140,12 @@
         send.wait()
 
 
-def pack_taps(values):
+def pack_taps(values, late):
     channels, length = values.shape
     view = tile_view(values)
     return pl.pallas_call(
         pack_taps_kernel,
-        in_specs=[HBM],
+        in_specs=[pl.BlockSpec(memory_space=pltpu.SMEM), HBM],
         out_specs=HBM,
         out_shape=jax.ShapeDtypeStruct((channels, length // LANES, LANES), F32),
         scratch_shapes=[
@@ -148,7 +154,7 @@
             pltpu.SemaphoreType.DMA((channels,)),
         ],
         name="pack_taps",
-    )(view)
+    )(late, view)
 
 
 def pack_kernel(src_ref, out_ref):
@@ -464,10 +470,12 @@
     shape = (blocks, ROWS // blocks, MIDS, LANES)
     tab = {k: jnp.asarray(v) for k, v in tables().items()}
 
+    late = (lax.axis_index("ch") % 2).astype(jnp.int32).reshape(1)
+
     def exchange(values):
         return lax.all_to_all(values.reshape(shape), "ctx", split_axis=0, concat_axis=0, tiled=True)
 
-    taps = pltpu.with_memory_space_constraint(exchange(pack_taps(filter_taps)), pltpu.VMEM)
+    taps = pltpu.with_memory_space_constraint(exchange(pack_taps(filter_taps, late)), pltpu.VMEM)
     skip = jnp.broadcast_to(skip_gain[:, None], (channels, LANES))
     packed, skip = lax.optimization_barrier((pack(signal), skip))
     values = exchange(packed)

time: 131 us -> 116 us (0.89); the launches traced: 129 us -> 116 us
  waiting for transfers between devices: 38.9 us -> 19.6 us
  Pallas kernels: 37.9 us -> 52.9 us
  blocking collectives: 33.7 us -> 25.4 us
    all_to_all x2, waiting for transfers between devices: 38.9 us -> 19.6 us  [exchange(): lax.all_to_all(values.reshape(shape), 'ctx', split_axis=0, concat_axis=0,...]
    pallas_call x1, Pallas kernels: 2.71 us -> 17.7 us  [pack_taps(): pl.pallas_call(pack_taps_kernel, in_specs=[pl.BlockSpec(memory_space=pltp...]
    all_to_all x1, blocking collectives: 33.7 us -> 25.4 us  [exchange(): lax.all_to_all(values.reshape(shape), 'ctx', split_axis=0, concat_axis=0,...]
  transfers between devices with their start and end apart: 2 -> 2, of which waited for: 2 -> 2; matrix products, arithmetic and copies ran while one was open for 0% -> 0% of each run, Pallas kernels for 13% -> 15%
where the time goes in v2:
time: 116 us
  Pallas kernels  52.9 us (46%)
  blocking collectives  25.4 us (22%)
  waiting for transfers between devices  19.6 us (17%)
  starting transfers between devices  17.8 us (15%)
    all_to_all x1, blocking collectives, exchange(): lax.all_to_all(values.reshape(shape), 'ctx', split_axis=0, concat_axis=0,...  25.4 us
    all_to_all x2, waiting for transfers between devices, exchange(): lax.all_to_all(values.reshape(shape), 'ctx', split_axis=0, concat_axis=0,...  19.6 us
    all_to_all x2, starting transfers between devices, exchange(): lax.all_to_all(values.reshape(shape), 'ctx', split_axis=0, concat_axis=0,...  17.8 us
    pallas_call x1, Pallas kernels, pack_taps(): pl.pallas_call(pack_taps_kernel, in_specs=[pl.BlockSpec(memory_space=pltp...  17.7 us
    pallas_call x1, Pallas kernels, convolve(): pl.pallas_call(convolve_kernel, in_specs=[ANY] + [HBM] * (1 + len(small))...  15.2 us
    pallas_call x1, Pallas kernels, transform_taps(): pl.pallas_call(taps_kernel, in_specs=[vmem] + [vmem] * len(names), out_sh...  13.7 us
    pallas_call x1, Pallas kernels, pack(): pl.pallas_call(pack_kernel, grid=(channels // block,), in_specs=[pl.Block...  3.26 us
    pallas_call x1, Pallas kernels, gate(): pl.pallas_call(gate_kernel, in_specs=[ANY, vmem, vmem, vmem], out_specs=H...  3.02 us
  transfers between devices with their start and end apart: 2, of which 2 were waited for; matrix products, arithmetic and copies ran while one was open for 0% of the time, Pallas kernels for 15%

profile of v2, /device:TPU:1, one launch (start us, length us, event | category | flops | bytes accessed | tf_op | source)
XLA Modules:
  0.0 115.9 jit_solution(6766567650459484713)
XLA Ops:
  0.0 17.7 %pack_taps.1 = f32[32,128,128]{2,1,0:T(8,128)} custom-call(s32[1]{0:T(128)} %bitcast.1.late_ref, f32[4,128,8,128]{3,2,1,0:T(8,128)} %bitcast.10), custom_call_target="tpu_custom_call" | custom-call | tf_op jit(solution)/shard_map/pack_taps/pallas_call | solution.py:146
  17.7 11.2 %all-to-all-start.1 = ((f32[32,8,16,128]{3,2,1,0:T(8,128)}), f32[32,8,16,128]{3,2,1,0:T(8,128)S(1)}, u32[]{:S(2)}, u32[]{:S(2)}) async-start(f32[32,8,16,128]{3,2,1,0:T(8,128)} %bitcast.9), calls=%async_computation.1 | async-start | bytes 4194304 | tf_op jit(solution)/shard_map/all_to_all | solution.py:476
  28.9 0.0 copy-start.2
  28.9 3.3 %pack.1 = f32[4096,128]{1,0:T(8,128)} custom-call(bf16[32,16384]{1,0:T(8,128)(2,1)} %signal_ref.1), custom_call_target="tpu_custom_call" | custom-call | tf_op jit(solution)/shard_map/pack/pallas_call | solution.py:173
  32.2 0.0 copy-done.2
  32.2 0.1 broadcast_in_dim.2.skip_ref
  32.3 15.0 %all-to-all-done.1.src_ref = f32[32,8,16,128]{3,2,1,0:T(8,128)S(1)} async-done(((f32[32,8,16,128]{3,2,1,0:T(8,128)}), f32[32,8,16,128]{3,2,1,0:T(8,128)S(1)}, u32[]{:S(2)}, u32[]{:S(2)}) %all-to-all-start.1) | async-done | bytes 2097184 | tf_op jit(solution)/shard_map/all_to_all | solution.py:476
  47.3 6.6 %all-to-all-start = ((f32[32,8,16,128]{3,2,1,0:T(8,128)}), f32[32,8,16,128]{3,2,1,0:T(8,128)}, u32[]{:S(2)}, u32[]{:S(2)}) async-start(f32[32,8,16,128]{3,2,1,0:T(8,128)} %bitcast.8), calls=%async_computation | async-start | bytes 4194304 | tf_op jit(solution)/shard_map/all_to_all | solution.py:476
  53.9 13.7 %taps.1.spec_ref = f32[16,256,256]{2,1,0:T(8,128)} custom-call(f32[32,8,16,128]{3,2,1,0:T(8,128)S(1)} %all-to-all-done.1.src_ref, bf16[512,256]{1,0:T(8,128)(2,1)} %constant.37.clone.first_hi.refs_0_, bf16[512,256]{1,0:T(8,128)(2,1)} %constant.38.clone.first_lo.refs_1_, bf16[256,256]{1,0:T(8,128)(2,1)} %constant.41.clone.third_hi.refs_4_, ...), custom_call_target="tpu_custom_call" | custom-call | tf_op jit(solution)/shard_map/taps/pallas_call | solution.py:428
  67.7 4.6 %all-to-all-done.src_ref = f32[32,8,16,128]{3,2,1,0:T(8,128)} async-done(((f32[32,8,16,128]{3,2,1,0:T(8,128)}), f32[32,8,16,128]{3,2,1,0:T(8,128)}, u32[]{:S(2)}, u32[]{:S(2)}) %all-to-all-start) | async-done | bytes 2097184 | tf_op jit(solution)/shard_map/all_to_all | solution.py:476
  72.2 15.2 %convolve.1 = f32[32,8,16,128]{3,2,1,0:T(8,128)} custom-call(f32[32,8,16,128]{3,2,1,0:T(8,128)} %all-to-all-done.src_ref, f32[16,256,256]{2,1,0:T(8,128)} %taps.1.spec_ref, bf16[512,256]{1,0:T(8,128)(2,1)} %constant.37.clone.first_hi.refs_0_, bf16[512,256]{1,0:T(8,128)(2,1)} %constant.38.clone.first_lo.refs_1_, bf16[512,512]{1,0:T(8,128)(2,1)} %constant.39.clone.refs_2_, ...), custom_call_target="tpu_custom_call" | custom-call | tf_op jit(solution)/shard_map/convolve/pallas_call | solution.py:446
  87.4 0.0 copy-start
  87.4 0.0 copy-start.1
  87.4 25.4 %all_to_all.15 = f32[32,8,16,128]{3,2,1,0:T(8,128)S(1)} all-to-all(f32[32,8,16,128]{3,2,1,0:T(8,128)} %convolve.1), channel_id=1, replica_groups=mesh['ctx'=32,'ch'=4] {'ctx'}, dimensions={0} | all-to-all | bytes 4194304 | tf_op jit(solution)/shard_map/all_to_all | solution.py:476
  112.9 0.0 copy-done
  112.9 0.0 copy-done.1
  112.9 3.0 %gate.1 = bf16[32,16384]{1,0:T(8,128)(2,1)} custom-call(f32[32,128,128]{2,1,0:T(8,128)S(1)} %bitcast.7, bf16[32,16384]{1,0:T(8,128)(2,1)S(1)} %copy-done, bf16[32,16384]{1,0:T(8,128)(2,1)S(1)} %copy-done.1, f32[32,128]{1,0:T(8,128)S(1)} %broadcast_in_dim.2.skip_ref), custom_call_target="tpu_custom_call" | custom-call | tf_op jit(solution)/shard_map/gate/pallas_call | solution.py:214
Async XLA Ops:
  17.7 29.6 %all-to-all-start.1 = ((f32[32,8,16,128]{3,2,1,0:T(8,128)}), f32[32,8,16,128]{3,2,1,0:T(8,128)S(1)}, u32[]{:S(2)}, u32[]{:S(2)}) async-start(f32[32,8,16,128]{3,2,1,0:T(8,128)} %bitcast.9), calls=%async_computation.1 | async-start | bytes 4194304 | tf_op jit(solution)/shard_map/all_to_all | solution.py:476
  28.9 3.3 %copy-start.2 = (f32[32]{0:T(128)S(1)}, f32[32]{0:T(128)}, u32[]{:S(2)}) copy-start(f32[32]{0:T(128)} %param.17) | copy-start | bytes 388
  47.3 25.0 %all-to-all-start = ((f32[32,8,16,128]{3,2,1,0:T(8,128)}), f32[32,8,16,128]{3,2,1,0:T(8,128)}, u32[]{:S(2)}, u32[]{:S(2)}) async-start(f32[32,8,16,128]{3,2,1,0:T(8,128)} %bitcast.8), calls=%async_computation | async-start | bytes 4194304 | tf_op jit(solution)/shard_map/all_to_all | solution.py:476
  87.4 25.5 %copy-start = (bf16[32,16384]{1,0:T(8,128)(2,1)S(1)}, bf16[32,16384]{1,0:T(8,128)(2,1)}, u32[]{:S(2)}) copy-start(bf16[32,16384]{1,0:T(8,128)(2,1)} %signal_ref.1) | copy-start | bytes 3145732
  87.4 25.4 %copy-start.1 = (bf16[32,16384]{1,0:T(8,128)(2,1)S(1)}, bf16[32,16384]{1,0:T(8,128)(2,1)}, u32[]{:S(2)}) copy-start(bf16[32,16384]{1,0:T(8,128)(2,1)} %gate_ref.1) | copy-start | bytes 3145732

commit v3 on v2

--- a/solution.py
+++ b/solution.py
@@ -102,6 +102,7 @@
 
 NEAR = LANES // MIDS
 STAGGER_NS = 15000
+UNROLL = 16
 BLOCK = 64
 HBM = pl.BlockSpec(memory_space=pltpu.HBM)
 ANY = pl.BlockSpec(memory_space=pl.ANY)
@@ -112,30 +113,42 @@
     return values.reshape(channels // 8, 8, length // LANES, LANES).transpose(0, 2, 1, 3)
 
 
-def send_chunks(buf, out_ref, sems, group):
-    copies = [
-        pltpu.make_async_copy(buf.at[group, :, c, :], out_ref.at[8 * group + c], sems.at[8 * group + c])
-        for c in range(8)
-    ]
-    for copy in copies:
-        copy.start()
-    return copies
-
-
-def pack_taps_kernel(late_ref, src_ref, out_ref, buf, in_sems, out_sems):
-    groups = src_ref.shape[0]
+def pack_taps_kernel(late_ref, src_ref, out_ref, buf, lines, in_sems, out_sems):
+    groups, rows = src_ref.shape[:2]
 
     @pl.when(late_ref[0] == 1)
     def _():
         pl.delay(STAGGER_NS)
 
     loads = [pltpu.make_async_copy(src_ref.at[g], buf.at[g], in_sems.at[g]) for g in range(groups)]
-    for load in loads:
-        load.start()
+    copied = range(groups // 2, groups)
+    for g in copied:
+        loads[g].start()
+    for g in range(groups // 2):
+        loads[g].start()
     sends = []
-    for g in range(groups):
+    for g in copied:
         loads[g].wait()
-        sends += send_chunks(buf, out_ref, out_sems, g)
+        for c in range(8):
+            channel = 8 * g + c
+            sends.append(pltpu.make_async_copy(buf.at[g, :, c, :], out_ref.at[channel], out_sems.at[channel]))
+            sends[-1].start()
+    for g in range(groups // 2):
+        loads[g].wait()
+
+        def spread(step, carry, g=g):
+            for i in range(UNROLL):
+                row = step * UNROLL + i
+                lines[pl.ds(8 * g * rows + row, 8, stride=rows), :] = buf[g, row]
+            return carry
+
+        lax.fori_loop(0, rows // UNROLL, spread, 0)
+        for c in range(8):
+            channel = 8 * g + c
+            sends.append(
+                pltpu.make_async_copy(lines.at[pl.ds(channel * rows, rows), :], out_ref.at[channel], out_sems.at[channel])
+            )
+            sends[-1].start()
     for send in sends:
         send.wait()
 
@@ -150,6 +163,7 @@
         out_shape=jax.ShapeDtypeStruct((channels, length // LANES, LANES), F32),
         scratch_shapes=[
             pltpu.VMEM(view.shape, F32),
+            pltpu.VMEM((channels // 2 * view.shape[1], LANES), F32),
             pltpu.SemaphoreType.DMA((channels // 8,)),
             pltpu.SemaphoreType.DMA((channels,)),
         ],
@@ -161,9 +175,16 @@
     channels, length = src_ref.shape
     rows = length // LANES
     for group in range(channels // 8):
-        for row in range(rows):
-            value = src_ref[pl.ds(8 * group, 8), pl.ds(row * LANES, LANES)].astype(F32)
-            out_ref[pl.ds(8 * group * rows + row, 8, stride=rows), :] = value
+
+        def spread(step, carry, group=group):
+            for i in range(UNROLL):
+                row = step * UNROLL + i
+                lanes = pl.ds(pl.multiple_of(row * LANES, LANES), LANES)
+                value = src_ref[pl.ds(8 * group, 8), lanes].astype(F32)
+                out_ref[pl.ds(8 * group * rows + row, 8, stride=rows), :] = value
+            return carry
+
+        lax.fori_loop(0, rows // UNROLL, spread, 0)
 
 
 def pack(values):
@@ -181,24 +202,36 @@
 
 
 def gate_kernel(conv_ref, signal_ref, gate_ref, skip_ref, out_ref, buf, out, sems, out_sems):
-    groups, rows = buf.shape[:2]
-    loads = [
-        pltpu.make_async_copy(conv_ref.at[8 * g + c], buf.at[g, :, c, :], sems.at[8 * g + c])
-        for g in range(groups)
+    groups = signal_ref.shape[0] // 8
+    rows = signal_ref.shape[1] // LANES
+    direct = groups - buf.shape[0]
+    loads = {
+        8 * g + c: pltpu.make_async_copy(
+            conv_ref.at[pl.ds((8 * g + c) * rows, rows), :], buf.at[g - direct, :, c, :], sems.at[8 * (g - direct) + c]
+        )
+        for g in range(direct, groups)
         for c in range(8)
-    ]
-    for load in loads:
+    }
+    for load in loads.values():
         load.start()
     stores = []
     for g in range(groups):
         lines = pl.ds(8 * g, 8)
         skip = skip_ref[lines, :]
-        for c in range(8):
-            loads[8 * g + c].wait()
-        for row in range(rows):
-            where = (lines, pl.ds(row * LANES, LANES))
-            total = buf[g, row] + skip * signal_ref[where].astype(F32)
-            out[where] = (gate_ref[where].astype(F32) * total).astype(BF16)
+        if g >= direct:
+            for c in range(8):
+                loads[8 * g + c].wait()
+
+        def some(step, carry, g=g, lines=lines, skip=skip):
+            for i in range(UNROLL):
+                row = step * UNROLL + i
+                where = (lines, pl.ds(pl.multiple_of(row * LANES, LANES), LANES))
+                conv = buf[g - direct, row] if g >= direct else conv_ref[pl.ds(8 * g * rows + row, 8, stride=rows), :]
+                total = conv + skip * signal_ref[where].astype(F32)
+                out[where] = (gate_ref[where].astype(F32) * total).astype(BF16)
+            return carry
+
+        lax.fori_loop(0, rows // UNROLL, some, 0)
         if g % 2:
             pair = pl.ds(8 * g - 8, 16)
             stores.append(pltpu.make_async_copy(out.at[pair, :], out_ref.at[pair, :], out_sems.at[g // 2]))
@@ -213,13 +246,13 @@
     vmem = pl.BlockSpec(memory_space=pltpu.VMEM)
     return pl.pallas_call(
         gate_kernel,
-        in_specs=[ANY, vmem, vmem, vmem],
+        in_specs=[vmem] * 4,
         out_specs=HBM,
         out_shape=jax.ShapeDtypeStruct((channels, length), BF16),
         scratch_shapes=[
-            pltpu.VMEM((channels // 8, rows, 8, LANES), F32),
+            pltpu.VMEM((channels // 16, rows, 8, LANES), F32),
             pltpu.VMEM((channels, length), BF16),
-            pltpu.SemaphoreType.DMA((channels,)),
+            pltpu.SemaphoreType.DMA((channels // 2,)),
             pltpu.SemaphoreType.DMA((channels // 16,)),
         ],
         compiler_params=pltpu.CompilerParams(vmem_limit_bytes=16 << 20),
@@ -312,15 +345,17 @@
 
     lax.fori_loop(0, ROWS // 8, mids, 0)
 
-    def step(k, carry):
-        values = jnp.concatenate([work_re[k], work_im[k]], axis=1)
-        out_ref[k] = lane_stage(values, third_hi, third_lo)
+    def step(j, carry):
+        rows = pl.ds(pl.multiple_of(j * BLOCK, BLOCK), BLOCK)
+        parts = [work[:, rows, :].reshape(MIDS * BLOCK, LANES) for work in (work_re, work_im)]
+        seen = lane_stage(jnp.concatenate(parts, axis=1), third_hi, third_lo)
+        out_ref[:, rows, :] = seen.reshape(MIDS, BLOCK, 2 * LANES)
         return carry
 
-    lax.fori_loop(0, MIDS, step, 0)
-
-
-SMALL = ("first_hi", "first_lo", "back", "back_hi", "third_hi", "third_lo", "undo_hi", "undo_lo", "mid", "twist")
+    lax.fori_loop(0, ROWS // BLOCK, step, 0)
+
+
+SMALL = ("first_hi", "first_lo", "back", "third_hi", "third_lo", "undo_hi", "undo_lo", "mid", "twist")
 
 
 def convolve_kernel(src_ref, spec_ref, *refs):
@@ -395,7 +430,7 @@
         )
         upper, lower = split(values)
         both = dot(tab["back"][...], upper)
-        result = both[:ROWS] + (both[ROWS:] + dot(tab["back_hi"][...], lower))
+        result = both[:ROWS] + (both[ROWS:] + dot(tab["back"][:ROWS], lower))
         for side in range(2):
             out[2 * pair + side] = result[:, side * LANES : (side + 1) * LANES].reshape(out.shape[1:])
             store(2 * pair + side).start()
@@ -413,7 +448,7 @@
     third_hi, third_lo = halves_of(third)
     undo_hi, undo_lo = halves_of(third.T.copy() / TOTAL)
     return dict(
-        first_hi=first_hi, first_lo=first_lo, back=np.concatenate([back_hi, back_lo], axis=0), back_hi=back_hi,
+        first_hi=first_hi, first_lo=first_lo, back=np.concatenate([back_hi, back_lo], axis=0),
         third_hi=third_hi, third_lo=third_lo, undo_hi=undo_hi, undo_lo=undo_lo, mid=mid, twist=twist,
     )
 
@@ -481,7 +516,7 @@
     values = exchange(packed)
     spectrum = transform_taps(taps, tab)
     conv = convolve(values, spectrum, tab)
-    back = exchange(conv).reshape(channels, length // LANES, LANES)
+    back = pltpu.with_memory_space_constraint(exchange(conv).reshape(channels * (length // LANES), LANES), pltpu.VMEM)
     return gate(back, signal, gate_values, skip)
 
 

time: 116 us -> 117 us (level)
  waiting for transfers between devices: 19.6 us -> 21.2 us
    pallas_call x1, Pallas kernels: 13.7 us -> 11.7 us  [transform_taps(): pl.pallas_call(taps_kernel, in_specs=[vmem] + [vmem] * len(names), out_sh...]
    all_to_all x2, waiting for transfers between devices: 19.6 us -> 21.2 us  [exchange(): lax.all_to_all(values.reshape(shape), 'ctx', split_axis=0, concat_axis=0,...]
  transfers between devices with their start and end apart: 2 -> 2, of which waited for: 2 -> 2; matrix products, arithmetic and copies ran while one was open for 0% -> 0% of each run, Pallas kernels for 15% -> 13%
where the time goes in v3:
time: 117 us; the launch traced here: 116 us
  Pallas kernels  51.8 us (44%)
  blocking collectives  25.4 us (22%)
  waiting for transfers between devices  21.2 us (18%)
  starting transfers between devices  17.8 us (15%)
    all_to_all x1, blocking collectives, exchange(): lax.all_to_all(values.reshape(shape), 'ctx', split_axis=0, concat_axis=0,...  25.4 us
    all_to_all x2, waiting for transfers between devices, exchange(): lax.all_to_all(values.reshape(shape), 'ctx', split_axis=0, concat_axis=0,...  21.2 us
    pallas_call x1, Pallas kernels, pack_taps(): pl.pallas_call(pack_taps_kernel, in_specs=[pl.BlockSpec(memory_space=pltp...  18.1 us
    all_to_all x2, starting transfers between devices, exchange(): lax.all_to_all(values.reshape(shape), 'ctx', split_axis=0, concat_axis=0,...  17.8 us
    pallas_call x1, Pallas kernels, convolve(): pl.pallas_call(convolve_kernel, in_specs=[ANY] + [HBM] * (1 + len(small))...  15.2 us
    pallas_call x1, Pallas kernels, transform_taps(): pl.pallas_call(taps_kernel, in_specs=[vmem] + [vmem] * len(names), out_sh...  11.7 us
    pallas_call x1, Pallas kernels, pack(): pl.pallas_call(pack_kernel, grid=(channels // block,), in_specs=[pl.Block...  3.66 us
    pallas_call x1, Pallas kernels, gate(): pl.pallas_call(gate_kernel, in_specs=[vmem] * 4, out_specs=HBM, out_shape...  3.14 us
  transfers between devices with their start and end apart: 2, of which 2 were waited for; matrix products, arithmetic and copies ran while one was open for 0% of the time, Pallas kernels for 13%

profile of v3, /device:TPU:1, one launch (start us, length us, event | category | flops | bytes accessed | tf_op | source)
XLA Modules:
  0.0 116.4 jit_solution(12847110293392288593)
XLA Ops:
  0.0 18.1 %pack_taps.1 = f32[32,128,128]{2,1,0:T(8,128)} custom-call(s32[1]{0:T(128)} %bitcast.1.late_ref, f32[4,128,8,128]{3,2,1,0:T(8,128)} %bitcast.10), custom_call_target="tpu_custom_call" | custom-call | tf_op jit(solution)/shard_map/pack_taps/pallas_call | solution.py:159
  18.1 11.2 %all-to-all-start.1 = ((f32[32,8,16,128]{3,2,1,0:T(8,128)}), f32[32,8,16,128]{3,2,1,0:T(8,128)S(1)}, u32[]{:S(2)}, u32[]{:S(2)}) async-start(f32[32,8,16,128]{3,2,1,0:T(8,128)} %bitcast.9), calls=%async_computation.1 | async-start | bytes 4194304 | tf_op jit(solution)/shard_map/all_to_all | solution.py:511
  29.3 0.0 copy-start.2
  29.3 3.7 %pack.1 = f32[4096,128]{1,0:T(8,128)} custom-call(bf16[32,16384]{1,0:T(8,128)(2,1)} %signal_ref.1), custom_call_target="tpu_custom_call" | custom-call | tf_op jit(solution)/shard_map/pack/pallas_call | solution.py:194
  33.0 0.0 copy-done.2
  33.0 0.1 broadcast_in_dim.2.skip_ref
  33.0 14.6 %all-to-all-done.1.src_ref = f32[32,8,16,128]{3,2,1,0:T(8,128)S(1)} async-done(((f32[32,8,16,128]{3,2,1,0:T(8,128)}), f32[32,8,16,128]{3,2,1,0:T(8,128)S(1)}, u32[]{:S(2)}, u32[]{:S(2)}) %all-to-all-start.1) | async-done | bytes 2097184 | tf_op jit(solution)/shard_map/all_to_all | solution.py:511
  47.7 6.6 %all-to-all-start = ((f32[32,8,16,128]{3,2,1,0:T(8,128)}), f32[32,8,16,128]{3,2,1,0:T(8,128)}, u32[]{:S(2)}, u32[]{:S(2)}) async-start(f32[32,8,16,128]{3,2,1,0:T(8,128)} %bitcast.8), calls=%async_computation | async-start | bytes 4194304 | tf_op jit(solution)/shard_map/all_to_all | solution.py:511
  54.3 11.7 %taps.1.spec_ref = f32[16,256,256]{2,1,0:T(8,128)} custom-call(f32[32,8,16,128]{3,2,1,0:T(8,128)S(1)} %all-to-all-done.1.src_ref, bf16[512,256]{1,0:T(8,128)(2,1)} %constant.35.clone.first_hi.refs_0_, bf16[512,256]{1,0:T(8,128)(2,1)} %constant.36.clone.first_lo.refs_1_, bf16[256,256]{1,0:T(8,128)(2,1)} %constant.38.clone.third_hi.refs_3_, ...), custom_call_target="tpu_custom_call" | custom-call | tf_op jit(solution)/shard_map/taps/pallas_call | solution.py:463
  66.1 6.6 %all-to-all-done.src_ref = f32[32,8,16,128]{3,2,1,0:T(8,128)} async-done(((f32[32,8,16,128]{3,2,1,0:T(8,128)}), f32[32,8,16,128]{3,2,1,0:T(8,128)}, u32[]{:S(2)}, u32[]{:S(2)}) %all-to-all-start) | async-done | bytes 2097184 | tf_op jit(solution)/shard_map/all_to_all | solution.py:511
  72.6 15.2 %convolve.1 = f32[32,8,16,128]{3,2,1,0:T(8,128)} custom-call(f32[32,8,16,128]{3,2,1,0:T(8,128)} %all-to-all-done.src_ref, f32[16,256,256]{2,1,0:T(8,128)} %taps.1.spec_ref, bf16[512,256]{1,0:T(8,128)(2,1)} %constant.35.clone.first_hi.refs_0_, bf16[512,256]{1,0:T(8,128)(2,1)} %constant.36.clone.first_lo.refs_1_, bf16[512,512]{1,0:T(8,128)(2,1)} %constant.37.clone.refs_2_, ...), custom_call_target="tpu_custom_call" | custom-call | tf_op jit(solution)/shard_map/convolve/pallas_call | solution.py:481
  87.8 0.0 copy-start
  87.9 0.0 copy-start.1
  87.9 25.4 %all_to_all.15 = f32[32,8,16,128]{3,2,1,0:T(8,128)S(1)} all-to-all(f32[32,8,16,128]{3,2,1,0:T(8,128)} %convolve.1), channel_id=1, replica_groups=mesh['ctx'=32,'ch'=4] {'ctx'}, dimensions={0} | all-to-all | bytes 4194304 | tf_op jit(solution)/shard_map/all_to_all | solution.py:511
  113.3 0.0 copy-done
  113.3 0.0 copy-done.1
  113.3 3.1 %gate.1 = bf16[32,16384]{1,0:T(8,128)(2,1)} custom-call(f32[4096,128]{1,0:T(8,128)S(1)} %bitcast.7, bf16[32,16384]{1,0:T(8,128)(2,1)S(1)} %copy-done, bf16[32,16384]{1,0:T(8,128)(2,1)S(1)} %copy-done.1, f32[32,128]{1,0:T(8,128)S(1)} %broadcast_in_dim.2.skip_ref), custom_call_target="tpu_custom_call" | custom-call | tf_op jit(solution)/shard_map/gate/pallas_call | solution.py:247
Async XLA Ops:
  18.1 29.6 %all-to-all-start.1 = ((f32[32,8,16,128]{3,2,1,0:T(8,128)}), f32[32,8,16,128]{3,2,1,0:T(8,128)S(1)}, u32[]{:S(2)}, u32[]{:S(2)}) async-start(f32[32,8,16,128]{3,2,1,0:T(8,128)} %bitcast.9), calls=%async_computation.1 | async-start | bytes 4194304 | tf_op jit(solution)/shard_map/all_to_all | solution.py:511
  29.3 3.7 %copy-start.2 = (f32[32]{0:T(128)S(1)}, f32[32]{0:T(128)}, u32[]{:S(2)}) copy-start(f32[32]{0:T(128)} %param.16) | copy-start | bytes 388
  47.7 25.0 %all-to-all-start = ((f32[32,8,16,128]{3,2,1,0:T(8,128)}), f32[32,8,16,128]{3,2,1,0:T(8,128)}, u32[]{:S(2)}, u32[]{:S(2)}) async-start(f32[32,8,16,128]{3,2,1,0:T(8,128)} %bitcast.8), calls=%async_computation | async-start | bytes 4194304 | tf_op jit(solution)/shard_map/all_to_all | solution.py:511
  87.8 25.4 %copy-start = (bf16[32,16384]{1,0:T(8,128)(2,1)S(1)}, bf16[32,16384]{1,0:T(8,128)(2,1)}, u32[]{:S(2)}) copy-start(bf16[32,16384]{1,0:T(8,128)(2,1)} %signal_ref.1) | copy-start | bytes 3145732
  87.9 25.4 %copy-start.1 = (bf16[32,16384]{1,0:T(8,128)(2,1)S(1)}, bf16[32,16384]{1,0:T(8,128)(2,1)}, u32[]{:S(2)}) copy-start(bf16[32,16384]{1,0:T(8,128)(2,1)} %gate_ref.1) | copy-start | bytes 3145732

commit v4 on v2

--- a/solution.py
+++ b/solution.py
@@ -112,18 +112,23 @@
     return values.reshape(channels // 8, 8, length // LANES, LANES).transpose(0, 2, 1, 3)
 
 
-def send_chunks(buf, out_ref, sems, group):
-    copies = [
-        pltpu.make_async_copy(buf.at[group, :, c, :], out_ref.at[8 * group + c], sems.at[8 * group + c])
-        for c in range(8)
-    ]
-    for copy in copies:
-        copy.start()
-    return copies
-
-
-def pack_taps_kernel(late_ref, src_ref, out_ref, buf, in_sems, out_sems):
-    groups = src_ref.shape[0]
+def swap_eight(tiles):
+    row = lax.broadcasted_iota(jnp.int32, tiles[0].shape, 0)
+    tiles = list(tiles)
+    for bit in (4, 2, 1):
+        odd = (row & bit) != 0
+        for low in range(8):
+            if low & bit:
+                continue
+            high = low | bit
+            first, second = tiles[low], tiles[high]
+            tiles[low] = jnp.where(odd, pltpu.roll(second, bit, 0), first)
+            tiles[high] = jnp.where(odd, second, pltpu.roll(first, 8 - bit, 0))
+    return tiles
+
+
+def pack_taps_kernel(late_ref, src_ref, out_ref, buf, lines, in_sems, out_sems):
+    groups, rows = src_ref.shape[:2]
 
     @pl.when(late_ref[0] == 1)
     def _():
@@ -135,7 +140,19 @@
     sends = []
     for g in range(groups):
         loads[g].wait()
-        sends += send_chunks(buf, out_ref, out_sems, g)
+
+        def spread(step, carry, g=g):
+            for part in range(2):
+                base = step * 16 + 8 * part
+                tiles = swap_eight([buf[g, base + i] for i in range(8)])
+                for c in range(8):
+                    lines[8 * g + c, pl.ds(pl.multiple_of(base, 8), 8), :] = tiles[c]
+            return carry
+
+        lax.fori_loop(0, rows // 16, spread, 0)
+        part = pl.ds(8 * g, 8)
+        sends.append(pltpu.make_async_copy(lines.at[part], out_ref.at[part], out_sems.at[g]))
+        sends[-1].start()
     for send in sends:
         send.wait()
 
@@ -150,8 +167,9 @@
         out_shape=jax.ShapeDtypeStruct((channels, length // LANES, LANES), F32),
         scratch_shapes=[
             pltpu.VMEM(view.shape, F32),
+            pltpu.VMEM((channels, length // LANES, LANES), F32),
             pltpu.SemaphoreType.DMA((channels // 8,)),
-            pltpu.SemaphoreType.DMA((channels,)),
+            pltpu.SemaphoreType.DMA((channels // 8,)),
         ],
         name="pack_taps",
     )(late, view)
@@ -180,25 +198,25 @@
     )(values)
 
 
-def gate_kernel(conv_ref, signal_ref, gate_ref, skip_ref, out_ref, buf, out, sems, out_sems):
-    groups, rows = buf.shape[:2]
-    loads = [
-        pltpu.make_async_copy(conv_ref.at[8 * g + c], buf.at[g, :, c, :], sems.at[8 * g + c])
-        for g in range(groups)
-        for c in range(8)
-    ]
-    for load in loads:
-        load.start()
+def gate_kernel(conv_ref, signal_ref, gate_ref, skip_ref, out_ref, out, out_sems):
+    channels, rows = conv_ref.shape[:2]
     stores = []
-    for g in range(groups):
+    for g in range(channels // 8):
         lines = pl.ds(8 * g, 8)
         skip = skip_ref[lines, :]
-        for c in range(8):
-            loads[8 * g + c].wait()
-        for row in range(rows):
-            where = (lines, pl.ds(row * LANES, LANES))
-            total = buf[g, row] + skip * signal_ref[where].astype(F32)
-            out[where] = (gate_ref[where].astype(F32) * total).astype(BF16)
+
+        def some(step, carry, g=g, lines=lines, skip=skip):
+            for part in range(2):
+                base = step * 16 + 8 * part
+                tiles = [conv_ref[8 * g + c, pl.ds(pl.multiple_of(base, 8), 8), :] for c in range(8)]
+                tiles = swap_eight(tiles)
+                for i in range(8):
+                    where = (lines, pl.ds(pl.multiple_of((base + i) * LANES, LANES), LANES))
+                    total = tiles[i] + skip * signal_ref[where].astype(F32)
+                    out[where] = (gate_ref[where].astype(F32) * total).astype(BF16)
+            return carry
+
+        lax.fori_loop(0, rows // 16, some, 0)
         if g % 2:
             pair = pl.ds(8 * g - 8, 16)
             stores.append(pltpu.make_async_copy(out.at[pair, :], out_ref.at[pair, :], out_sems.at[g // 2]))
@@ -209,17 +227,14 @@
 
 def gate(conv, signal, gate_values, skip):
     channels, length = signal.shape
-    rows = length // LANES
     vmem = pl.BlockSpec(memory_space=pltpu.VMEM)
     return pl.pallas_call(
         gate_kernel,
-        in_specs=[ANY, vmem, vmem, vmem],
+        in_specs=[vmem] * 4,
         out_specs=HBM,
         out_shape=jax.ShapeDtypeStruct((channels, length), BF16),
         scratch_shapes=[
-            pltpu.VMEM((channels // 8, rows, 8, LANES), F32),
             pltpu.VMEM((channels, length), BF16),
-            pltpu.SemaphoreType.DMA((channels,)),
             pltpu.SemaphoreType.DMA((channels // 16,)),
         ],
         compiler_params=pltpu.CompilerParams(vmem_limit_bytes=16 << 20),
@@ -312,15 +327,17 @@
 
     lax.fori_loop(0, ROWS // 8, mids, 0)
 
-    def step(k, carry):
-        values = jnp.concatenate([work_re[k], work_im[k]], axis=1)
-        out_ref[k] = lane_stage(values, third_hi, third_lo)
+    def step(j, carry):
+        rows = pl.ds(pl.multiple_of(j * BLOCK, BLOCK), BLOCK)
+        parts = [work[:, rows, :].reshape(MIDS * BLOCK, LANES) for work in (work_re, work_im)]
+        seen = lane_stage(jnp.concatenate(parts, axis=1), third_hi, third_lo)
+        out_ref[:, rows, :] = seen.reshape(MIDS, BLOCK, 2 * LANES)
         return carry
 
-    lax.fori_loop(0, MIDS, step, 0)
-
-
-SMALL = ("first_hi", "first_lo", "back", "back_hi", "third_hi", "third_lo", "undo_hi", "undo_lo", "mid", "twist")
+    lax.fori_loop(0, ROWS // BLOCK, step, 0)
+
+
+SMALL = ("first_hi", "first_lo", "back", "third_hi", "third_lo", "undo_hi", "undo_lo", "mid", "twist")
 
 
 def convolve_kernel(src_ref, spec_ref, *refs):
@@ -395,7 +412,7 @@
         )
         upper, lower = split(values)
         both = dot(tab["back"][...], upper)
-        result = both[:ROWS] + (both[ROWS:] + dot(tab["back_hi"][...], lower))
+        result = both[:ROWS] + (both[ROWS:] + dot(tab["back"][:ROWS], lower))
         for side in range(2):
             out[2 * pair + side] = result[:, side * LANES : (side + 1) * LANES].reshape(out.shape[1:])
             store(2 * pair + side).start()
@@ -413,7 +430,7 @@
     third_hi, third_lo = halves_of(third)
     undo_hi, undo_lo = halves_of(third.T.copy() / TOTAL)
     return dict(
-        first_hi=first_hi, first_lo=first_lo, back=np.concatenate([back_hi, back_lo], axis=0), back_hi=back_hi,
+        first_hi=first_hi, first_lo=first_lo, back=np.concatenate([back_hi, back_lo], axis=0),
         third_hi=third_hi, third_lo=third_lo, undo_hi=undo_hi, undo_lo=undo_lo, mid=mid, twist=twist,
     )
 
@@ -481,7 +498,7 @@
     values = exchange(packed)
     spectrum = transform_taps(taps, tab)
     conv = convolve(values, spectrum, tab)
-    back = exchange(conv).reshape(channels, length // LANES, LANES)
+    back = pltpu.with_memory_space_constraint(exchange(conv).reshape(channels, length // LANES, LANES), pltpu.VMEM)
     return gate(back, signal, gate_values, skip)
 
 

time: 116 us -> 115 us (level)
  Pallas kernels: 52.9 us -> 49.7 us
  waiting for transfers between devices: 19.6 us -> 21.6 us
    pallas_call x1, Pallas kernels: 13.7 us -> 11.7 us  [transform_taps(): pl.pallas_call(taps_kernel, in_specs=[vmem] + [vmem] * len(names), out_sh...]
    all_to_all x2, waiting for transfers between devices: 19.6 us -> 21.6 us  [exchange(): lax.all_to_all(values.reshape(shape), 'ctx', split_axis=0, concat_axis=0,...]
  transfers between devices with their start and end apart: 2 -> 2, of which waited for: 2 -> 2; matrix products, arithmetic and copies ran while one was open for 0% -> 0% of each run, Pallas kernels for 15% -> 13%
where the time goes in v4:
time: 115 us
  Pallas kernels  49.7 us (43%)
  blocking collectives  25.4 us (22%)
  waiting for transfers between devices  21.6 us (19%)
  starting transfers between devices  17.8 us (15%)
    all_to_all x1, blocking collectives, exchange(): lax.all_to_all(values.reshape(shape), 'ctx', split_axis=0, concat_axis=0,...  25.4 us
    all_to_all x2, waiting for transfers between devices, exchange(): lax.all_to_all(values.reshape(shape), 'ctx', split_axis=0, concat_axis=0,...  21.6 us
    all_to_all x2, starting transfers between devices, exchange(): lax.all_to_all(values.reshape(shape), 'ctx', split_axis=0, concat_axis=0,...  17.8 us
    pallas_call x1, Pallas kernels, pack_taps(): pl.pallas_call(pack_taps_kernel, in_specs=[pl.BlockSpec(memory_space=pltp...  17.6 us
    pallas_call x1, Pallas kernels, convolve(): pl.pallas_call(convolve_kernel, in_specs=[ANY] + [HBM] * (1 + len(small))...  15.2 us
    pallas_call x1, Pallas kernels, transform_taps(): pl.pallas_call(taps_kernel, in_specs=[vmem] + [vmem] * len(names), out_sh...  11.7 us
    pallas_call x1, Pallas kernels, pack(): pl.pallas_call(pack_kernel, grid=(channels // block,), in_specs=[pl.Block...  3.26 us
  transfers between devices with their start and end apart: 2, of which 2 were waited for; matrix products, arithmetic and copies ran while one was open for 0% of the time, Pallas kernels for 13%

profile of v4, /device:TPU:1, one launch (start us, length us, event | category | flops | bytes accessed | tf_op | source)
XLA Modules:
  0.0 114.7 jit_solution(946334508869800437)
XLA Ops:
  0.0 17.6 %pack_taps.1 = f32[32,128,128]{2,1,0:T(8,128)} custom-call(s32[1]{0:T(128)} %bitcast.1.late_ref, f32[4,128,8,128]{3,2,1,0:T(8,128)} %bitcast.10), custom_call_target="tpu_custom_call" | custom-call | tf_op jit(solution)/shard_map/pack_taps/pallas_call | solution.py:163
  17.6 11.2 %all-to-all-start.1 = ((f32[32,8,16,128]{3,2,1,0:T(8,128)}), f32[32,8,16,128]{3,2,1,0:T(8,128)S(1)}, u32[]{:S(2)}, u32[]{:S(2)}) async-start(f32[32,8,16,128]{3,2,1,0:T(8,128)} %bitcast.9), calls=%async_computation.1 | async-start | bytes 4194304 | tf_op jit(solution)/shard_map/all_to_all | solution.py:493
  28.8 0.0 copy-start.2
  28.8 3.3 %pack.1 = f32[4096,128]{1,0:T(8,128)} custom-call(bf16[32,16384]{1,0:T(8,128)(2,1)} %signal_ref.1), custom_call_target="tpu_custom_call" | custom-call | tf_op jit(solution)/shard_map/pack/pallas_call | solution.py:191
  32.1 0.0 copy-done.2
  32.1 0.1 broadcast_in_dim.2.skip_ref
  32.1 15.0 %all-to-all-done.1.src_ref = f32[32,8,16,128]{3,2,1,0:T(8,128)S(1)} async-done(((f32[32,8,16,128]{3,2,1,0:T(8,128)}), f32[32,8,16,128]{3,2,1,0:T(8,128)S(1)}, u32[]{:S(2)}, u32[]{:S(2)}) %all-to-all-start.1) | async-done | bytes 2097184 | tf_op jit(solution)/shard_map/all_to_all | solution.py:493
  47.2 6.6 %all-to-all-start = ((f32[32,8,16,128]{3,2,1,0:T(8,128)}), f32[32,8,16,128]{3,2,1,0:T(8,128)}, u32[]{:S(2)}, u32[]{:S(2)}) async-start(f32[32,8,16,128]{3,2,1,0:T(8,128)} %bitcast.8), calls=%async_computation | async-start | bytes 4194304 | tf_op jit(solution)/shard_map/all_to_all | solution.py:493
  53.8 11.7 %taps.1.spec_ref = f32[16,256,256]{2,1,0:T(8,128)} custom-call(f32[32,8,16,128]{3,2,1,0:T(8,128)S(1)} %all-to-all-done.1.src_ref, bf16[512,256]{1,0:T(8,128)(2,1)} %constant.35.clone.first_hi.refs_0_, bf16[512,256]{1,0:T(8,128)(2,1)} %constant.36.clone.first_lo.refs_1_, bf16[256,256]{1,0:T(8,128)(2,1)} %constant.38.clone.third_hi.refs_3_, ...), custom_call_target="tpu_custom_call" | custom-call | tf_op jit(solution)/shard_map/taps/pallas_call | solution.py:445
  65.6 6.6 %all-to-all-done.src_ref = f32[32,8,16,128]{3,2,1,0:T(8,128)} async-done(((f32[32,8,16,128]{3,2,1,0:T(8,128)}), f32[32,8,16,128]{3,2,1,0:T(8,128)}, u32[]{:S(2)}, u32[]{:S(2)}) %all-to-all-start) | async-done | bytes 2097184 | tf_op jit(solution)/shard_map/all_to_all | solution.py:493
  72.1 15.2 %convolve.1 = f32[32,8,16,128]{3,2,1,0:T(8,128)} custom-call(f32[32,8,16,128]{3,2,1,0:T(8,128)} %all-to-all-done.src_ref, f32[16,256,256]{2,1,0:T(8,128)} %taps.1.spec_ref, bf16[512,256]{1,0:T(8,128)(2,1)} %constant.35.clone.first_hi.refs_0_, bf16[512,256]{1,0:T(8,128)(2,1)} %constant.36.clone.first_lo.refs_1_, bf16[512,512]{1,0:T(8,128)(2,1)} %constant.37.clone.refs_2_, ...), custom_call_target="tpu_custom_call" | custom-call | tf_op jit(solution)/shard_map/convolve/pallas_call | solution.py:463
  87.3 0.0 copy-start
  87.3 0.0 copy-start.1
  87.4 25.4 %all_to_all.15 = f32[32,8,16,128]{3,2,1,0:T(8,128)S(1)} all-to-all(f32[32,8,16,128]{3,2,1,0:T(8,128)} %convolve.1), channel_id=1, replica_groups=mesh['ctx'=32,'ch'=4] {'ctx'}, dimensions={0} | all-to-all | bytes 4194304 | tf_op jit(solution)/shard_map/all_to_all | solution.py:493
  112.8 0.0 copy-done
  112.8 0.0 copy-done.1
  112.8 1.9 %gate.1 = bf16[32,16384]{1,0:T(8,128)(2,1)} custom-call(f32[32,128,128]{2,1,0:T(8,128)S(1)} %bitcast.7, bf16[32,16384]{1,0:T(8,128)(2,1)S(1)} %copy-done, bf16[32,16384]{1,0:T(8,128)(2,1)S(1)} %copy-done.1, f32[32,128]{1,0:T(8,128)S(1)} %broadcast_in_dim.2.skip_ref), custom_call_target="tpu_custom_call" | custom-call | tf_op jit(solution)/shard_map/gate/pallas_call | solution.py:231
Async XLA Ops:
  17.6 29.6 %all-to-all-start.1 = ((f32[32,8,16,128]{3,2,1,0:T(8,128)}), f32[32,8,16,128]{3,2,1,0:T(8,128)S(1)}, u32[]{:S(2)}, u32[]{:S(2)}) async-start(f32[32,8,16,128]{3,2,1,0:T(8,128)} %bitcast.9), calls=%async_computation.1 | async-start | bytes 4194304 | tf_op jit(solution)/shard_map/all_to_all | solution.py:493
  28.8 3.3 %copy-start.2 = (f32[32]{0:T(128)S(1)}, f32[32]{0:T(128)}, u32[]{:S(2)}) copy-start(f32[32]{0:T(128)} %param.16) | copy-start | bytes 388
  47.2 25.0 %all-to-all-start = ((f32[32,8,16,128]{3,2,1,0:T(8,128)}), f32[32,8,16,128]{3,2,1,0:T(8,128)}, u32[]{:S(2)}, u32[]{:S(2)}) async-start(f32[32,8,16,128]{3,2,1,0:T(8,128)} %bitcast.8), calls=%async_computation | async-start | bytes 4194304 | tf_op jit(solution)/shard_map/all_to_all | solution.py:493
  87.3 25.5 %copy-start = (bf16[32,16384]{1,0:T(8,128)(2,1)S(1)}, bf16[32,16384]{1,0:T(8,128)(2,1)}, u32[]{:S(2)}) copy-start(bf16[32,16384]{1,0:T(8,128)(2,1)} %signal_ref.1) | copy-start | bytes 3145732
  87.3 25.4 %copy-start.1 = (bf16[32,16384]{1,0:T(8,128)(2,1)S(1)}, bf16[32,16384]{1,0:T(8,128)(2,1)}, u32[]{:S(2)}) copy-start(bf16[32,16384]{1,0:T(8,128)(2,1)} %gate_ref.1) | copy-start | bytes 3145732

commit v5 on v4

--- a/solution.py
+++ b/solution.py
@@ -101,7 +101,7 @@
 
 
 NEAR = LANES // MIDS
-STAGGER_NS = 15000
+STAGGER_NS = 15300
 BLOCK = 64
 HBM = pl.BlockSpec(memory_space=pltpu.HBM)
 ANY = pl.BlockSpec(memory_space=pl.ANY)

time: 115 us -> 114 us (level)
  blocking collectives: 25.4 us -> 23.7 us
    all_to_all x1, blocking collectives: 25.4 us -> 23.7 us  [exchange(): lax.all_to_all(values.reshape(shape), 'ctx', split_axis=0, concat_axis=0,...]
where the time goes in v5:
time: 114 us
  Pallas kernels  50.1 us (44%)
  blocking collectives  23.7 us (21%)
  waiting for transfers between devices  22 us (19%)
  starting transfers between devices  18 us (16%)
    all_to_all x1, blocking collectives, exchange(): lax.all_to_all(values.reshape(shape), 'ctx', split_axis=0, concat_axis=0,...  23.7 us
    all_to_all x2, waiting for transfers between devices, exchange(): lax.all_to_all(values.reshape(shape), 'ctx', split_axis=0, concat_axis=0,...  22 us
    all_to_all x2, starting transfers between devices, exchange(): lax.all_to_all(values.reshape(shape), 'ctx', split_axis=0, concat_axis=0,...  18 us
    pallas_call x1, Pallas kernels, pack_taps(): pl.pallas_call(pack_taps_kernel, in_specs=[pl.BlockSpec(memory_space=pltp...  17.9 us
    pallas_call x1, Pallas kernels, convolve(): pl.pallas_call(convolve_kernel, in_specs=[ANY] + [HBM] * (1 + len(small))...  15.3 us
    pallas_call x1, Pallas kernels, transform_taps(): pl.pallas_call(taps_kernel, in_specs=[vmem] + [vmem] * len(names), out_sh...  11.7 us
    pallas_call x1, Pallas kernels, pack(): pl.pallas_call(pack_kernel, grid=(channels // block,), in_specs=[pl.Block...  3.26 us
  transfers between devices with their start and end apart: 2, of which 2 were waited for; matrix products, arithmetic and copies ran while one was open for 0% of the time, Pallas kernels for 13%

profile of v5, /device:TPU:1, one launch (start us, length us, event | category | flops | bytes accessed | tf_op | source)
XLA Modules:
  0.0 114.0 jit_solution(1393893516076963241)
XLA Ops:
  0.0 17.9 %pack_taps.1 = f32[32,128,128]{2,1,0:T(8,128)} custom-call(s32[1]{0:T(128)} %bitcast.1.late_ref, f32[4,128,8,128]{3,2,1,0:T(8,128)} %bitcast.10), custom_call_target="tpu_custom_call" | custom-call | tf_op jit(solution)/shard_map/pack_taps/pallas_call | solution.py:163
  17.9 11.2 %all-to-all-start.1 = ((f32[32,8,16,128]{3,2,1,0:T(8,128)}), f32[32,8,16,128]{3,2,1,0:T(8,128)S(1)}, u32[]{:S(2)}, u32[]{:S(2)}) async-start(f32[32,8,16,128]{3,2,1,0:T(8,128)} %bitcast.9), calls=%async_computation.1 | async-start | bytes 4194304 | tf_op jit(solution)/shard_map/all_to_all | solution.py:493
  29.1 0.0 copy-start.2
  29.1 3.3 %pack.1 = f32[4096,128]{1,0:T(8,128)} custom-call(bf16[32,16384]{1,0:T(8,128)(2,1)} %signal_ref.1), custom_call_target="tpu_custom_call" | custom-call | tf_op jit(solution)/shard_map/pack/pallas_call | solution.py:191
  32.4 0.0 copy-done.2
  32.4 0.1 broadcast_in_dim.2.skip_ref
  32.4 15.4 %all-to-all-done.1.src_ref = f32[32,8,16,128]{3,2,1,0:T(8,128)S(1)} async-done(((f32[32,8,16,128]{3,2,1,0:T(8,128)}), f32[32,8,16,128]{3,2,1,0:T(8,128)S(1)}, u32[]{:S(2)}, u32[]{:S(2)}) %all-to-all-start.1) | async-done | bytes 2097184 | tf_op jit(solution)/shard_map/all_to_all | solution.py:493
  47.9 6.8 %all-to-all-start = ((f32[32,8,16,128]{3,2,1,0:T(8,128)}), f32[32,8,16,128]{3,2,1,0:T(8,128)}, u32[]{:S(2)}, u32[]{:S(2)}) async-start(f32[32,8,16,128]{3,2,1,0:T(8,128)} %bitcast.8), calls=%async_computation | async-start | bytes 4194304 | tf_op jit(solution)/shard_map/all_to_all | solution.py:493
  54.7 11.7 %taps.1.spec_ref = f32[16,256,256]{2,1,0:T(8,128)} custom-call(f32[32,8,16,128]{3,2,1,0:T(8,128)S(1)} %all-to-all-done.1.src_ref, bf16[512,256]{1,0:T(8,128)(2,1)} %constant.35.clone.first_hi.refs_0_, bf16[512,256]{1,0:T(8,128)(2,1)} %constant.36.clone.first_lo.refs_1_, bf16[256,256]{1,0:T(8,128)(2,1)} %constant.38.clone.third_hi.refs_3_, ...), custom_call_target="tpu_custom_call" | custom-call | tf_op jit(solution)/shard_map/taps/pallas_call | solution.py:445
  66.4 6.6 %all-to-all-done.src_ref = f32[32,8,16,128]{3,2,1,0:T(8,128)} async-done(((f32[32,8,16,128]{3,2,1,0:T(8,128)}), f32[32,8,16,128]{3,2,1,0:T(8,128)}, u32[]{:S(2)}, u32[]{:S(2)}) %all-to-all-start) | async-done | bytes 2097184 | tf_op jit(solution)/shard_map/all_to_all | solution.py:493
  73.0 15.3 %convolve.1 = f32[32,8,16,128]{3,2,1,0:T(8,128)} custom-call(f32[32,8,16,128]{3,2,1,0:T(8,128)} %all-to-all-done.src_ref, f32[16,256,256]{2,1,0:T(8,128)} %taps.1.spec_ref, bf16[512,256]{1,0:T(8,128)(2,1)} %constant.35.clone.first_hi.refs_0_, bf16[512,256]{1,0:T(8,128)(2,1)} %constant.36.clone.first_lo.refs_1_, bf16[512,512]{1,0:T(8,128)(2,1)} %constant.37.clone.refs_2_, ...), custom_call_target="tpu_custom_call" | custom-call | tf_op jit(solution)/shard_map/convolve/pallas_call | solution.py:463
  88.3 0.0 copy-start
  88.3 0.0 copy-start.1
  88.3 23.7 %all_to_all.15 = f32[32,8,16,128]{3,2,1,0:T(8,128)S(1)} all-to-all(f32[32,8,16,128]{3,2,1,0:T(8,128)} %convolve.1), channel_id=1, replica_groups=mesh['ctx'=32,'ch'=4] {'ctx'}, dimensions={0} | all-to-all | bytes 4194304 | tf_op jit(solution)/shard_map/all_to_all | solution.py:493
  112.1 0.0 copy-done
  112.1 0.0 copy-done.1
  112.1 1.9 %gate.1 = bf16[32,16384]{1,0:T(8,128)(2,1)} custom-call(f32[32,128,128]{2,1,0:T(8,128)S(1)} %bitcast.7, bf16[32,16384]{1,0:T(8,128)(2,1)S(1)} %copy-done, bf16[32,16384]{1,0:T(8,128)(2,1)S(1)} %copy-done.1, f32[32,128]{1,0:T(8,128)S(1)} %broadcast_in_dim.2.skip_ref), custom_call_target="tpu_custom_call" | custom-call | tf_op jit(solution)/shard_map/gate/pallas_call | solution.py:231
Async XLA Ops:
  17.9 29.9 %all-to-all-start.1 = ((f32[32,8,16,128]{3,2,1,0:T(8,128)}), f32[32,8,16,128]{3,2,1,0:T(8,128)S(1)}, u32[]{:S(2)}, u32[]{:S(2)}) async-start(f32[32,8,16,128]{3,2,1,0:T(8,128)} %bitcast.9), calls=%async_computation.1 | async-start | bytes 4194304 | tf_op jit(solution)/shard_map/all_to_all | solution.py:493
  29.1 3.3 %copy-start.2 = (f32[32]{0:T(128)S(1)}, f32[32]{0:T(128)}, u32[]{:S(2)}) copy-start(f32[32]{0:T(128)} %param.16) | copy-start | bytes 388
  47.9 25.1 %all-to-all-start = ((f32[32,8,16,128]{3,2,1,0:T(8,128)}), f32[32,8,16,128]{3,2,1,0:T(8,128)}, u32[]{:S(2)}, u32[]{:S(2)}) async-start(f32[32,8,16,128]{3,2,1,0:T(8,128)} %bitcast.8), calls=%async_computation | async-start | bytes 4194304 | tf_op jit(solution)/shard_map/all_to_all | solution.py:493
  88.3 23.8 %copy-start = (bf16[32,16384]{1,0:T(8,128)(2,1)S(1)}, bf16[32,16384]{1,0:T(8,128)(2,1)}, u32[]{:S(2)}) copy-start(bf16[32,16384]{1,0:T(8,128)(2,1)} %signal_ref.1) | copy-start | bytes 3145732
  88.3 23.7 %copy-start.1 = (bf16[32,16384]{1,0:T(8,128)(2,1)S(1)}, bf16[32,16384]{1,0:T(8,128)(2,1)}, u32[]{:S(2)}) copy-start(bf16[32,16384]{1,0:T(8,128)(2,1)} %gate_ref.1) | copy-start | bytes 3145732
